TPU v7x, 256 devices: a whole 4x4x8 slice. The times are simulated.
256 devices in a mesh: group: 4 (over y), dev: 64 (over z, x, core).
Axes of the slice: x: 4, y: 4, z: 8, core: 2. Of those that a mesh axis runs over, the one named last changes fastest.
Arguments:
- source_emb: float32 [2048, 128, 128], P(('group', 'dev')), may hold values from -6 to 6
- target_emb: float32 [8192, 128, 128], P(('group', 'dev')), may hold values from -6 to 6
- source_mass: float32 [2048, 128], P(('group', 'dev')), may hold values from 0.5 to 2
- target_mass: float32 [8192, 128], P(('group', 'dev')), may hold values from 0.5 to 2
- cand_device: int32 [2048, 7], P(('group', 'dev')), may hold values from 0 to 63, all different within a row; in each aligned block of 8 rows (0 to 7, 8 to 15, ...) at most 2 rows name the same one
- cand_block: int32 [2048, 8], P(('group', 'dev')), may hold values from 0 to 31
Outputs:
- src_scale: float32 [2048, 128], P(('group', 'dev'))
- tgt_scale: float32 [8192, 128], P(('group', 'dev'))
Inputs may be any that keep to these rules, and one draw needn't show every extreme that they name: `cand_device`: the seven devices named by one source block are distinct; among the 8 source blocks of one device, no device is named more than 2 times, and some device is named exactly 2 times.
All inputs are finite; a program needn't handle non-finite values.
Results may differ from a plain program's by a relative error of at most 0.0001.
Values sent between devices are 32-bit elements; how exact they have to be, the bound alone decides.
A program may use at most 64 MiB of HBM per device.

v0:
```python
import jax
import jax.numpy as jnp
from jax import lax
from jax.sharding import PartitionSpec as P

NODE_GROUP_SIZE = 128
FEATURE_LENGTH = 128
ITERS = 2


entropic_regularizer = 0.1
dustbin = 0.5
epsilon = 1e-06


def from_behind(x, axis, by):
    count = lax.axis_size(axis)
    return lax.ppermute(x, axis, [(i, (i + by) % count) for i in range(count)])


def unit_rows(emb):
    return emb * lax.rsqrt(jnp.mean(emb * emb, axis=-1, keepdims=True) + epsilon)


def selected_rows(table, asked_rows, dev_count, slot_cap):
    picked = jnp.take(table, asked_rows, axis=0)
    return picked.reshape((dev_count, slot_cap) + table.shape[1:])


def assemble(nearby_flattened, far_part, slot_index, sb_dev, near_count):
    near_part = jnp.take(nearby_flattened, slot_index, axis=0).reshape(
        (sb_dev, near_count) + nearby_flattened.shape[1:]
    )
    return jnp.concatenate([near_part, far_part[:, None]], axis=1)


def build_kernel(src_unit, pair_emb):
    alignment_affinity = jnp.einsum(
        "ibd,ikjd->ikbj", src_unit, pair_emb, precision=lax.Precision.HIGHEST
    )
    return jnp.exp(alignment_affinity * (1.0 / (FEATURE_LENGTH * entropic_regularizer))) / (
        8.0 * NODE_GROUP_SIZE
    )


def local(source_emb, target_emb, source_mass, target_mass, cand_device, cand_block):
    dev_count = lax.axis_size("dev")
    sb_dev = source_emb.shape[0]
    tb_dev = target_emb.shape[0]
    near_count = cand_device.shape[1]
    slot_cap = (near_count * sb_dev + dev_count - 1) // dev_count + 1
    count_of_pairs = sb_dev * near_count
    src_unit = unit_rows(source_emb)
    tgt_unit = unit_rows(target_emb)
    target_dev = cand_device.reshape(count_of_pairs)
    onehot = (target_dev[:, None] == jnp.arange(dev_count, dtype=jnp.int32)[None, :]).astype(
        jnp.int32
    )
    before = jnp.cumsum(onehot, axis=0) - onehot
    position_rank = jnp.sum(before * onehot, axis=1)
    slot_index = target_dev * slot_cap + position_rank
    wanted = (
        jnp.zeros((dev_count * slot_cap,), jnp.int32)
        .at[slot_index]
        .set(cand_block[:, :near_count].reshape(count_of_pairs))
    )
    asked_rows = lax.all_to_all(
        wanted.reshape(dev_count, slot_cap), "dev", split_axis=0, concat_axis=0, tiled=True
    ).reshape(dev_count * slot_cap)
    owner_hot = (asked_rows[:, None] == jnp.arange(tb_dev, dtype=jnp.int32)[None, :]).astype(
        jnp.float32
    )
    remote_node_group = cand_block[:, near_count]
    twin_hot = (remote_node_group[:, None] == jnp.arange(tb_dev, dtype=jnp.int32)[None, :]).astype(
        jnp.float32
    )
    twin_emb = from_behind(tgt_unit, "group", -1)
    far_emb = jnp.take(twin_emb, remote_node_group, axis=0)
    tgt_scale = jnp.ones_like(target_mass)
    src_scale = jnp.ones_like(source_mass)
    kernel = None
    for sweep in range(ITERS):
        if sweep == 0:
            far_scale = jnp.ones((sb_dev, target_mass.shape[1]), jnp.float32)
        else:
            twin_scale = from_behind(tgt_scale, "group", -1)
            far_scale = jnp.take(twin_scale, remote_node_group, axis=0)
        fetched_emb, fetched_scale = (
            lax.all_to_all(
                selected_rows(tgt_unit, asked_rows, dev_count, slot_cap),
                "dev",
                split_axis=0,
                concat_axis=0,
                tiled=True,
            ),
            lax.all_to_all(
                selected_rows(tgt_scale, asked_rows, dev_count, slot_cap),
                "dev",
                split_axis=0,
                concat_axis=0,
                tiled=True,
            ),
        )
        fetched_emb = fetched_emb.reshape((dev_count * slot_cap,) + tgt_unit.shape[1:])
        near_scale = fetched_scale.reshape(dev_count * slot_cap, target_mass.shape[1])
        kernel = build_kernel(
            src_unit, assemble(fetched_emb, far_emb, slot_index, sb_dev, near_count)
        )
        pair_scale = assemble(near_scale, far_scale, slot_index, sb_dev, near_count)
        row_sums = jnp.einsum("ikbj,ikj->ib", kernel, pair_scale, precision=lax.Precision.HIGHEST)
        src_scale = source_mass / (dustbin + row_sums)
        col_parts = jnp.einsum("ikbj,ib->ikj", kernel, src_scale, precision=lax.Precision.HIGHEST)
        departing_messages = jnp.zeros((dev_count * slot_cap, col_parts.shape[2]), jnp.float32)
        departing_messages = departing_messages.at[slot_index].set(
            col_parts[:, :near_count].reshape(count_of_pairs, col_parts.shape[2])
        )
        arrived = lax.all_to_all(
            departing_messages.reshape(dev_count, slot_cap, col_parts.shape[2]),
            "dev",
            split_axis=0,
            concat_axis=0,
            tiled=True,
        )
        arrived = arrived.reshape(dev_count * slot_cap, col_parts.shape[2])
        col_sums = jnp.einsum("sn,sb->nb", owner_hot, arrived, precision=lax.Precision.HIGHEST)
        twin_parts = jnp.einsum(
            "sn,sb->nb", twin_hot, col_parts[:, near_count], precision=lax.Precision.HIGHEST
        )
        col_sums = col_sums + from_behind(twin_parts, "group", 1)
        tgt_scale = target_mass / (dustbin + col_sums)
    return (src_scale, tgt_scale)


def solution(mesh):
    placed = (
        P(("group", "dev"), None, None),
        P(("group", "dev"), None, None),
        P(("group", "dev"), None),
        P(("group", "dev"), None),
        P(("group", "dev"), None),
        P(("group", "dev"), None),
    )
    return jax.shard_map(
        local,
        mesh=mesh,
        in_specs=placed,
        out_specs=(P(("group", "dev"), None), P(("group", "dev"), None)),
        check_vma=False,
    )
```

profile of v0, /device:TPU:1, one launch (start us, length us, event | category | flops | bytes accessed | tf_op | source)
XLA Modules:
  0.0 325.0 jit_solution(14148153204652474383)
XLA Ops:
  0.6 0.7 broadcast_multiply_fusion.1
  1.3 0.8 eq.43
  2.1 0.1 mul.55
  2.2 0.1 fusion.27
  2.2 0.1 reduce_window_sum.11
  2.3 0.2 select_reduce_fusion
  2.5 0.8 reshape.258
  3.3 0.7 scatter_custom_fusion
  4.0 0.7 all_to_all.22
  4.8 13.0 %all-to-all-start = ((s32[64,1,2]{2,1,0:T(1,128)}), s32[64,1,2]{2,1,0:T(1,128)S(1)}, u32[]{:S(2)}, u32[]{:S(2)}) async-start(s32[64,1,2]{2,1,0:T(1,128)} %bitcast.2), calls=%async_computation | async-start | bytes 65536 | tf_op jit(solution)/shard_map/all_to_all | solution.py:67
  17.8 2.2 multiply_reduce_fusion
  20.0 2.2 broadcast_multiply_fusion
  22.2 5.0 %all-to-all-done = s32[64,1,2]{2,1,0:T(1,128)S(1)} async-done(((s32[64,1,2]{2,1,0:T(1,128)}), s32[64,1,2]{2,1,0:T(1,128)S(1)}, u32[]{:S(2)}, u32[]{:S(2)}) %all-to-all-start) | async-done | bytes 544 | tf_op jit(solution)/shard_map/all_to_all | solution.py:67
  27.2 0.5 broadcast.201
  27.7 0.7 reduce.9
  28.4 0.1 reshape.174
  28.6 0.6 gather_fusion.4
  29.3 0.7 broadcast_select_fusion.3
  30.0 5.3 %all-to-all-start.2 = ((f32[64,2,128]{2,1,0:T(2,128)}), f32[64,2,128]{2,1,0:T(2,128)S(1)}, u32[]{:S(2)}, u32[]{:S(2)}) async-start(f32[64,2,128]{2,1,0:T(2,128)} %bitcast.10), calls=%async_computation.2 | async-start | bytes 131072 | tf_op jit(solution)/shard_map/all_to_all | solution.py:96
  35.3 4.3 %gather_fusion.2 = f32[128,128,128]{2,1,0:T(8,128)} fusion(f32[32,128,128]{2,1,0:T(8,128)S(1)} %broadcast_multiply_fusion, s32[1024]{0:T(1024)S(1)} %pad_clamp_fusion.2), kind=kCustom, calls=%fused_computation.clone | custom fusion | bytes 16777728 | tf_op jit(solution)/shard_map/jit(_take)/gather | solution.py:26
  39.6 7.2 %broadcast_select_fusion = f32[128,128,128]{2,1,0:T(8,128)} fusion(f32[128,128,128]{2,1,0:T(8,128)} %gather_fusion.2, pred[128]{0:T(512)(128)(4,1)S(1)} %compare_and_fusion.1), kind=kLoop, calls=%fused_computation.23 | loop fusion | flops 2097152 | bytes 16777344 | tf_op jit(solution)/shard_map/jit(_take)/select_n | solution.py:26
  46.8 10.6 %all-to-all-start.1 = ((f32[64,2,128,128]{3,2,1,0:T(8,128)}), f32[64,2,128,128]{3,2,1,0:T(8,128)}, u32[]{:S(2)}, u32[]{:S(2)}) async-start(f32[64,2,128,128]{3,2,1,0:T(8,128)} %bitcast.72), calls=%async_computation.1 | async-start | bytes 16777216 | tf_op jit(solution)/shard_map/all_to_all | solution.py:89
  57.5 3.0 collective-permute-start
  60.5 0.2 slice_reduce_fusion
  60.7 0.2 and_reduce_fusion
  60.9 0.2 multiply_reduce_fusion.1
  61.1 0.6 gather_fusion.5
  61.7 0.1 broadcast_select_fusion.5
  61.8 43.1 %collective-permute-done = f32[32,128,128]{2,1,0:T(8,128)} collective-permute-done((f32[32,128,128]{2,1,0:T(8,128)S(1)}, f32[32,128,128]{2,1,0:T(8,128)}, u32[]{:S(2)}, u32[]{:S(2)}) %collective-permute-start) | collective-permute-done | bytes 2097184 | tf_op jit(solution)/shard_map/ppermute | solution.py:18
  104.9 2.2 gather_fusion
  107.1 0.1 bitcast_select_fusion
  107.2 132.6 %all-to-all-done.1 = f32[64,2,128,128]{3,2,1,0:T(8,128)} async-done(((f32[64,2,128,128]{3,2,1,0:T(8,128)}), f32[64,2,128,128]{3,2,1,0:T(8,128)}, u32[]{:S(2)}, u32[]{:S(2)}) %all-to-all-start.1) | async-done | bytes 8388640 | tf_op jit(solution)/shard_map/all_to_all | solution.py:89
  239.7 6.0 %gather_fusion.3 = f32[56,128,128]{2,1,0:T(8,128)} fusion(f32[128,128,128]{2,1,0:T(8,128)} %bitcast.4, s32[1024]{0:T(1024)S(1)} %pad_clamp_fusion.1), kind=kCustom, calls=%fused_computation.1.clone | custom fusion | bytes 7340256 | tf_op jit(solution)/shard_map/jit(_take)/gather | solution.py:31
  245.8 2.3 broadcast_select_fusion.1
  248.1 4.7 %exponential_multiply_fusion = f32[8,8,128,128]{3,2,1,0:T(8,128)S(1)} fusion(f32[8,1,128,128]{3,2,1,0:T(8,128)S(1)} %bitcast_select_fusion, f32[8,7,128,128]{3,2,1,0:T(8,128)S(1)} %bitcast.73, f32[8,128,128]{2,1,0:T(8,128)S(1)} %copy-done.2, f32[8,128]{1,0:T(8,128)S(1)} %add_rsqrt_fusion.1), kind=kOutput, calls=%fused_computation.24 | convolution fusion | flops 1613889536 | bytes 8916992 | tf_op jit(solution)/shard_map/ibd,ikjd->ikbj/dot_general | solution.py:38
  252.8 0.0 copy-start.6
  252.8 0.0 copy-start.3
  252.8 2.3 fusion.10
  255.2 3.6 %fusion.8 = f32[8,1,8,128]{3,1,2,0:T(1,128)S(1)} fusion(f32[8,128,1,1]{1,2,3,0:T(1,128)S(1)} %bitcast.87, f32[8,8,128,128]{3,2,1,0:T(8,128)S(1)} %exponential_multiply_fusion), kind=kOutput, calls=%fused_computation.19 | convolution fusion | flops 12582912 | bytes 4231168 | tf_op jit(solution)/shard_map/ikbj,ib->ikj/dot_general | solution.py:112
  258.8 1.3 scatter_custom_fusion.1
  260.1 10.1 %all-to-all-start.3 = ((f32[64,2,128]{2,1,0:T(2,128)}), f32[64,2,128]{2,1,0:T(2,128)S(1)}, u32[]{:S(2)}, u32[]{:S(2)}) async-start(f32[64,2,128]{2,1,0:T(2,128)} %bitcast.20), calls=%async_computation.3 | async-start | bytes 131072 | tf_op jit(solution)/shard_map/all_to_all | solution.py:117
  270.2 0.3 fusion.29
  270.5 1.6 collective-permute-start.1
  272.1 2.9 collective-permute-done.1
  274.9 5.4 %all-to-all-done.3 = f32[64,2,128]{2,1,0:T(2,128)S(1)} async-done(((f32[64,2,128]{2,1,0:T(2,128)}), f32[64,2,128]{2,1,0:T(2,128)S(1)}, u32[]{:S(2)}, u32[]{:S(2)}) %all-to-all-start.3) | async-done | bytes 65568 | tf_op jit(solution)/shard_map/all_to_all | solution.py:117
  280.3 0.3 fusion.17
  280.6 2.8 collective-permute-start.2
  283.4 0.6 gather_fusion.6
  284.1 0.7 broadcast_select_fusion.2
  284.8 4.8 %all-to-all-start.4 = ((f32[64,2,128]{2,1,0:T(2,128)}), f32[64,2,128]{2,1,0:T(2,128)S(1)}, u32[]{:S(2)}, u32[]{:S(2)}) async-start(f32[64,2,128]{2,1,0:T(2,128)} %bitcast.23), calls=%async_computation.4 | async-start | bytes 131072 | tf_op jit(solution)/shard_map/all_to_all | solution.py:96
  289.6 0.6 gather_fusion.1
  290.1 0.1 bitcast_select_fusion.1
  290.2 9.4 %all-to-all-done.4 = f32[64,2,128]{2,1,0:T(2,128)S(1)} async-done(((f32[64,2,128]{2,1,0:T(2,128)}), f32[64,2,128]{2,1,0:T(2,128)S(1)}, u32[]{:S(2)}, u32[]{:S(2)}) %all-to-all-start.4) | async-done | bytes 65568 | tf_op jit(solution)/shard_map/all_to_all | solution.py:96
  299.6 0.6 gather_fusion.7
  300.2 0.1 broadcast_select_fusion.4
  300.3 4.2 %fusion.6 = f32[8,1,128,1]{2,1,3,0:T(1,128)S(1)} fusion(f32[8,8,128,1]{2,3,1,0:T(1,128)S(1)} %bitcast.83, f32[8,8,128,128]{3,2,1,0:T(8,128)} %copy-done), kind=kOutput, calls=%fused_computation.17 | convolution fusion | flops 12582912 | bytes 4231168 | tf_op jit(solution)/shard_map/ikbj,ikj->ib/dot_general | solution.py:110
  304.6 3.6 %fusion.4 = f32[8,1,8,128]{3,1,2,0:T(1,128)S(1)} fusion(f32[8,128,1,1]{1,2,3,0:T(1,128)S(1)} %bitcast.85, f32[8,8,128,128]{3,2,1,0:T(8,128)S(1)} %copy-done.1), kind=kOutput, calls=%fused_computation.15 | convolution fusion | flops 12582912 | bytes 4231168 | tf_op jit(solution)/shard_map/ikbj,ib->ikj/dot_general | solution.py:112
  308.2 1.3 scatter_custom_fusion.2
  309.5 4.4 %all-to-all-start.5 = ((f32[64,2,128]{2,1,0:T(2,128)}), f32[64,2,128]{2,1,0:T(2,128)S(1)}, u32[]{:S(2)}, u32[]{:S(2)}) async-start(f32[64,2,128]{2,1,0:T(2,128)} %bitcast.35), calls=%async_computation.5 | async-start | bytes 131072 | tf_op jit(solution)/shard_map/all_to_all | solution.py:117
  314.0 0.3 fusion.28
  314.2 0.1 collective-permute-start.3
  314.3 4.1 %collective-permute-done.3 = f32[32,128]{1,0:T(8,128)S(1)} collective-permute-done((f32[32,128]{1,0:T(8,128)S(1)}, f32[32,128]{1,0:T(8,128)S(1)}, u32[]{:S(2)}, u32[]{:S(2)}) %collective-permute-start.3) | collective-permute-done | bytes 16416 | tf_op jit(solution)/shard_map/ppermute | solution.py:18
  318.4 5.7 %all-to-all-done.5 = f32[64,2,128]{2,1,0:T(2,128)S(1)} async-done(((f32[64,2,128]{2,1,0:T(2,128)}), f32[64,2,128]{2,1,0:T(2,128)S(1)}, u32[]{:S(2)}, u32[]{:S(2)}) %all-to-all-start.5) | async-done | bytes 65568 | tf_op jit(solution)/shard_map/all_to_all | solution.py:117
  324.1 0.9 fusion.15
  (34 shorter events, 0.2 us)
Async XLA Ops:
  4.8 22.4 %all-to-all-start = ((s32[64,1,2]{2,1,0:T(1,128)}), s32[64,1,2]{2,1,0:T(1,128)S(1)}, u32[]{:S(2)}, u32[]{:S(2)}) async-start(s32[64,1,2]{2,1,0:T(1,128)} %bitcast.2), calls=%async_computation | async-start | bytes 65536 | tf_op jit(solution)/shard_map/all_to_all | solution.py:67
  30.0 16.9 %all-to-all-start.2 = ((f32[64,2,128]{2,1,0:T(2,128)}), f32[64,2,128]{2,1,0:T(2,128)S(1)}, u32[]{:S(2)}, u32[]{:S(2)}) async-start(f32[64,2,128]{2,1,0:T(2,128)} %bitcast.10), calls=%async_computation.2 | async-start | bytes 131072 | tf_op jit(solution)/shard_map/all_to_all | solution.py:96
  46.8 13.6 %copy-start.4 = (s32[8,8]{1,0:T(8,128)S(1)}, s32[8,8]{1,0:T(8,128)}, u32[]{:S(2)}) copy-start(s32[8,8]{1,0:T(8,128)} %param.19) | copy-start | bytes 772
  46.8 14.0 %copy-start.2 = (f32[8,128,128]{2,1,0:T(8,128)S(1)}, f32[8,128,128]{2,1,0:T(8,128)}, u32[]{:S(2)}) copy-start(f32[8,128,128]{2,1,0:T(8,128)} %param.14) | copy-start | bytes 1572868
  46.8 192.9 %all-to-all-start.1 = ((f32[64,2,128,128]{3,2,1,0:T(8,128)}), f32[64,2,128,128]{3,2,1,0:T(8,128)}, u32[]{:S(2)}, u32[]{:S(2)}) async-start(f32[64,2,128,128]{3,2,1,0:T(8,128)} %bitcast.72), calls=%async_computation.1 | async-start | bytes 16777216 | tf_op jit(solution)/shard_map/all_to_all | solution.py:89
  57.5 47.4 %collective-permute-start = (f32[32,128,128]{2,1,0:T(8,128)S(1)}, f32[32,128,128]{2,1,0:T(8,128)}, u32[]{:S(2)}, u32[]{:S(2)}) collective-permute-start(f32[32,128,128]{2,1,0:T(8,128)S(1)} %broadcast_multiply_fusion), channel_id=1, source_target_pairs={{0,192},{64,0},{128,64},{192,128},{1,193},{65,1},{129,65},{193,129... | collective-permute-start | bytes 6291464 | tf_op jit(solution)/shard_map/ppermute | solution.py:18
  252.8 6.0 %copy-start = (f32[8,8,128,128]{3,2,1,0:T(8,128)}, f32[8,8,128,128]{3,2,1,0:T(8,128)S(1)}, u32[]{:S(2)}) copy-start(f32[8,8,128,128]{3,2,1,0:T(8,128)S(1)} %exponential_multiply_fusion) | copy-start | bytes 12582916
  252.8 2.3 copy-start.6
  252.8 27.5 %copy-start.3 = (f32[32,128]{1,0:T(8,128)S(1)}, f32[32,128]{1,0:T(8,128)}, u32[]{:S(2)}) copy-start(f32[32,128]{1,0:T(8,128)} %param.17) | copy-start | bytes 49156
  260.1 20.2 %all-to-all-start.3 = ((f32[64,2,128]{2,1,0:T(2,128)}), f32[64,2,128]{2,1,0:T(2,128)S(1)}, u32[]{:S(2)}, u32[]{:S(2)}) async-start(f32[64,2,128]{2,1,0:T(2,128)} %bitcast.20), calls=%async_computation.3 | async-start | bytes 131072 | tf_op jit(solution)/shard_map/all_to_all | solution.py:117
  270.5 4.5 %collective-permute-start.1 = (f32[32,128]{1,0:T(8,128)S(1)}, f32[32,128]{1,0:T(8,128)S(1)}, u32[]{:S(2)}, u32[]{:S(2)}) collective-permute-start(f32[32,128]{1,0:T(8,128)S(1)} %fusion.29), channel_id=1, source_target_pairs={{0,64},{64,128},{128,192},{192,0},{1,65},{65,129},{129,193},{193,1... | collective-permute-start | bytes 49160 | tf_op jit(solution)/shard_map/ppermute | solution.py:18
  280.6 9.0 %collective-permute-start.2 = (f32[32,128]{1,0:T(8,128)S(1)}, f32[32,128]{1,0:T(8,128)S(1)}, u32[]{:S(2)}, u32[]{:S(2)}) collective-permute-start(f32[32,128]{1,0:T(8,128)S(1)} %fusion.17), channel_id=1, source_target_pairs={{0,192},{64,0},{128,64},{192,128},{1,193},{65,1},{129,65},{193,129... | collective-permute-start | bytes 49160 | tf_op jit(solution)/shard_map/ppermute | solution.py:18
  284.8 14.8 %all-to-all-start.4 = ((f32[64,2,128]{2,1,0:T(2,128)}), f32[64,2,128]{2,1,0:T(2,128)S(1)}, u32[]{:S(2)}, u32[]{:S(2)}) async-start(f32[64,2,128]{2,1,0:T(2,128)} %bitcast.23), calls=%async_computation.4 | async-start | bytes 131072 | tf_op jit(solution)/shard_map/all_to_all | solution.py:96
  300.3 4.3 %copy-start.1 = (f32[8,8,128,128]{3,2,1,0:T(8,128)S(1)}, f32[8,8,128,128]{3,2,1,0:T(8,128)}, u32[]{:S(2)}) copy-start(f32[8,8,128,128]{3,2,1,0:T(8,128)} %copy-done) | copy-start | bytes 12582916
  304.6 20.4 %copy-start.5 = (f32[8,128]{1,0:T(8,128)}, f32[8,128]{1,0:T(8,128)S(1)}, u32[]{:S(2)}) copy-start(f32[8,128]{1,0:T(8,128)S(1)} %add_divide_fusion) | copy-start | bytes 12292
  309.5 14.6 %all-to-all-start.5 = ((f32[64,2,128]{2,1,0:T(2,128)}), f32[64,2,128]{2,1,0:T(2,128)S(1)}, u32[]{:S(2)}, u32[]{:S(2)}) async-start(f32[64,2,128]{2,1,0:T(2,128)} %bitcast.35), calls=%async_computation.5 | async-start | bytes 131072 | tf_op jit(solution)/shard_map/all_to_all | solution.py:117
  314.2 4.2 %collective-permute-start.3 = (f32[32,128]{1,0:T(8,128)S(1)}, f32[32,128]{1,0:T(8,128)S(1)}, u32[]{:S(2)}, u32[]{:S(2)}) collective-permute-start(f32[32,128]{1,0:T(8,128)S(1)} %fusion.28), channel_id=1, source_target_pairs={{0,64},{64,128},{128,192},{192,0},{1,65},{65,129},{129,193},{193,1... | collective-permute-start | bytes 49160 | tf_op jit(solution)/shard_map/ppermute | solution.py:18
where the time goes:
time: 326 us; the launch traced here: 325 us
  waiting for transfers between devices  208 us (64%)
  starting transfers between devices  55.7 us (17%)
  local copies, waits for them, and re-layouts  22 us (7%)
  matrix products  20.1 us (6%)
  other arithmetic  18.1 us (6%)
    all_to_all x1, waiting for transfers between devices, local(): lax.all_to_all(selected_rows(tgt_unit, asked_rows, dev_count, slot_cap),...  133 us
    ppermute x4, waiting for transfers between devices, from_behind(): return lax.ppermute(x, axis, [(i, (i + by) % count) for i in range(count)])  50.1 us
    all_to_all x2, starting transfers between devices, local(): lax.all_to_all(departing_messages.reshape(dev_count, slot_cap, col_parts....  14.5 us
    all_to_all x1, starting transfers between devices, local(): lax.all_to_all(wanted.reshape(dev_count, slot_cap), 'dev', split_axis=0,...  13 us
    all_to_all x2, waiting for transfers between devices, local(): lax.all_to_all(departing_messages.reshape(dev_count, slot_cap, col_parts....  11 us
    all_to_all x1, starting transfers between devices, local(): lax.all_to_all(selected_rows(tgt_unit, asked_rows, dev_count, slot_cap),...  10.6 us
    all_to_all x2, starting transfers between devices, local(): lax.all_to_all(selected_rows(tgt_scale, asked_rows, dev_count, slot_cap),...  10.1 us
    all_to_all x2, waiting for transfers between devices, local(): lax.all_to_all(selected_rows(tgt_scale, asked_rows, dev_count, slot_cap),...  9.41 us
  transfers between devices with their start and end apart: 10, of which 8 were waited for; matrix products, arithmetic and copies ran while one was open for 7% of the time, Pallas kernels for 0%

commit v1 on v0

v1 whole, which is shorter than its diff:
```python
import functools

import jax
import jax.numpy as jnp
from jax import lax
from jax.experimental import pallas as pl
from jax.experimental.pallas import tpu as pltpu
from jax.sharding import PartitionSpec as P

MESH = pl.DeviceIdType.MESH
N = 128
NX = 4
NEAR = 7
CAP = 2
ITERS = 2
EMPTY = -64
CHUNK = 8
DUSTBIN = 0.5
EPSILON = 1e-6
GAIN = 1.0 / (N * 0.1)
SHARE = 1.0 / (8.0 * N)

F32, BF16, I32 = jnp.float32, jnp.bfloat16, jnp.int32


def nt(a, b):
    return lax.dot_general(a, b, (((1,), (1,)), ((), ())), preferred_element_type=F32)


def nn(a, b):
    return lax.dot_general(a, b, (((1,), (0,)), ((), ())), preferred_element_type=F32)


def halves(v):
    hi = v.astype(BF16).astype(F32)
    return hi, v - hi


def kernel(ng, nz, sb, tb_dev, *refs):
    (semb, temb, smass, tmass, cdev, cblk, src_out, tgt_out,
     s_raw, t_raw, f_raw, s_hi, s_lo, t_hi, t_lo, f_hi, f_lo, k_hi, k_lo, kf_hi, kf_lo,
     tab, tabs, tabf, tabs_sm, tabf_sm,
     rp0, rp1, rpi0, rpi1, rf0, rf1, rfi0, rfi1, so0, so1, ss0, ss1, sf0, sf1,
     co0, co1, ci0, ci1, to, ts, snd, rcv, loc) = refs
    nr = 2 * nz
    hops = nz // 2
    half = sb // 2
    g, d = lax.axis_index("group"), lax.axis_index("dev")
    z, x, c = d // (2 * NX), (d // 2) % NX, d % 2

    def dev(dz, dx, flip):
        zz, xx = lax.rem(z + dz, nz), lax.rem(x + dx, NX)
        return (g, zz * (2 * NX) + xx * 2 + (1 - c if flip else c))

    def rel(dz, flip):
        return (dz % nz) * 2 + flip

    up, down = dev(1, 0, 0), dev(nz - 1, 0, 0)
    right, left = dev(0, 1, 0), dev(0, NX - 1, 0)
    partner = dev(0, 0, 1)
    ahead, behind = (lax.rem(g + 1, ng), d), (lax.rem(g + ng - 1, ng), d)

    count = [0]
    sent = []

    def send(src, dst, to_dev):
        k = count[0]
        count[0] += 1
        copy = pltpu.make_async_remote_copy(
            src_ref=src, dst_ref=dst, send_sem=snd.at[k], recv_sem=rcv.at[k],
            device_id=to_dev, device_id_type=MESH)
        copy.start()
        sent.append(copy)
        return copy

    barrier = pltpu.get_barrier_semaphore()
    greeted = (up, down, right, left, partner, ahead, behind)
    for other in greeted:
        pl.semaphore_signal(barrier, inc=1, device_id=other, device_id_type=MESH)
    own_s = pltpu.make_async_copy(semb, s_raw.at[0], loc.at[0])
    own_t = pltpu.make_async_copy(temb, t_raw.at[0], loc.at[1])
    own_s.start()
    own_t.start()

    lane = lax.broadcasted_iota(I32, (1, N), 1)
    run = jnp.zeros((1, N), I32)
    rows = [jnp.full((1, N), EMPTY, I32) for _ in range(2 * CAP)]
    far = jnp.zeros((1, N), I32)
    for b in range(sb):
        hit = jnp.zeros((1, N), I32)
        which = jnp.zeros((1, N), I32)
        for k in range(NEAR):
            m = cdev[b : b + 1, k : k + 1] == lane
            hit = jnp.where(m, 1, hit)
            which = jnp.where(m, cblk[b : b + 1, k : k + 1], which)
        for u in range(CAP):
            m = (hit == 1) & (run == u)
            rows[u] = jnp.where(m, b, rows[u])
            rows[CAP + u] = jnp.where(m, which, rows[CAP + u])
        run = run + hit
        far = jnp.where(lane == b, cblk[b : b + 1, NEAR : NEAR + 1], far)
    table = jnp.concatenate(rows + [far] + [jnp.zeros((1, N), I32)] * (7 - 2 * CAP), axis=0)
    tab[...] = table
    tabs[0] = table

    pl.semaphore_wait(barrier, len(greeted))

    chunks = tb_dev // CHUNK
    mid = chunks // 2
    t_plus, t_minus = {}, {}
    minus_order = list(range(mid, chunks)) + list(range(mid))
    for i in range(chunks):
        p, m = pl.ds(i * CHUNK, CHUNK), pl.ds(minus_order[i] * CHUNK, CHUNK)
        t_plus[i] = send(temb.at[p], t_raw.at[NX - 1, p], right)
        t_minus[minus_order[i]] = send(temb.at[m], t_raw.at[1, m], left)
    w_far = send(tab, tabf, ahead)
    f_far = send(semb, f_raw, ahead)

    w_mate = {0: send(tab, tabs.at[rel(0, 1)], partner)}
    w_plus = {1: send(tab, tabs.at[rel(-1, 0)], up)}
    w_minus = {1: send(tab, tabs.at[rel(1, 0)], down)}
    for h in range(2, hops + 2):
        if h - 1 in w_plus:
            w_plus[h - 1].wait_recv()
            if h <= hops:
                w_plus[h] = send(tabs.at[rel(1 - h, 0)], tabs.at[rel(-h, 0)], up)
            w_mate[-(h - 1)] = send(tabs.at[rel(1 - h, 0)], tabs.at[rel(1 - h, 1)], partner)
        if h - 1 in w_minus:
            w_minus[h - 1].wait_recv()
            if h <= hops - 1:
                w_minus[h] = send(tabs.at[rel(h - 1, 0)], tabs.at[rel(h, 0)], down)
            w_mate[h - 1] = send(tabs.at[rel(h - 1, 0)], tabs.at[rel(h - 1, 1)], partner)

    s_plus = {1: send(semb, s_raw.at[rel(-1, 0)], up)}
    s_minus = {1: send(semb, s_raw.at[rel(1, 0)], down)}
    s_mate = {0: send(semb, s_raw.at[rel(0, 1)], partner)}

    def normalize(raw, hi, lo, start, size, into):
        def one(i, _):
            v = raw[start + i]
            v = v * lax.rsqrt(jnp.mean(v * v, axis=-1, keepdims=True) + EPSILON)
            h = v.astype(BF16)
            hi[into + i] = h
            lo[into + i] = (v - h.astype(F32)).astype(BF16)
            return 0

        lax.fori_loop(0, size, one, 0)

    def norm_s(dz, flip):
        r = rel(dz, flip)
        normalize(s_raw.at[r], s_hi, s_lo, 0, sb, r * sb)

    def norm_t(t, start, size):
        normalize(t_raw.at[t], t_hi.at[t], t_lo.at[t], start, size, start)

    for w in w_mate.values():
        w.wait_recv()
    tables = pltpu.make_async_copy(tabs, tabs_sm, loc.at[2])
    tables.start()
    own_s.wait()
    norm_s(0, 0)
    own_t.wait()
    norm_t(0, 0, tb_dev)
    relay_plus, relay_minus = {}, {}
    for h in range(1, hops + 1):
        if h <= chunks:
            i, j = h - 1, minus_order[h - 1]
            pi, pj = pl.ds(i * CHUNK, CHUNK), pl.ds(j * CHUNK, CHUNK)
            t_plus[i].wait_recv()
            if i < mid:
                relay_plus[i] = send(t_raw.at[NX - 1, pi], t_raw.at[2, pi], right)
            t_minus[j].wait_recv()
            if j >= mid:
                relay_minus[j] = send(t_raw.at[1, pj], t_raw.at[2, pj], left)
        s_plus[h].wait_recv()
        s_minus[h].wait_recv()
        a, b = rel(-h, 0), rel(h, 0)
        if h + 1 < hops:
            s_plus[h + 1] = send(s_raw.at[a], s_raw.at[rel(-h - 1, 0)], up)
            s_minus[h + 1] = send(s_raw.at[b], s_raw.at[rel(h + 1, 0)], down)
        elif h + 1 == hops:
            lo_half, hi_half = pl.ds(0, half), pl.ds(half, half)
            last = rel(hops, 0)
            s_plus[hops] = send(s_raw.at[a, lo_half], s_raw.at[last, lo_half], up)
            s_minus[hops] = send(s_raw.at[b, hi_half], s_raw.at[last, hi_half], down)
        if h < hops:
            s_mate[-h] = send(s_raw.at[a], s_raw.at[rel(-h, 1)], partner)
            s_mate[h] = send(s_raw.at[b], s_raw.at[rel(h, 1)], partner)
            norm_s(-h, 0)
            norm_s(h, 0)
        else:
            s_mate[h] = send(s_raw.at[a], s_raw.at[rel(h, 1)], partner)
            norm_s(h, 0)
        if h <= chunks:
            norm_t(NX - 1, i * CHUNK, CHUNK)
            norm_t(1, j * CHUNK, CHUNK)
        if h == 1:
            f_far.wait_recv()
            w_far.wait_recv()
            far_table = pltpu.make_async_copy(tabf, tabf_sm, loc.at[3])
            far_table.start()
            normalize(f_raw, f_hi, f_lo, 0, sb, 0)
            tables.wait()
            far_table.wait()
    for dz, copy in s_mate.items():
        copy.wait_recv()
        norm_s(dz, 1)

    sub16 = lax.broadcasted_iota(I32, (16, N), 0)
    sub32 = lax.broadcasted_iota(I32, (tb_dev, N), 0)

    def lane_of(t):
        return z * (2 * NX) + lax.rem(x + t, NX) * 2 + c

    def tile(a_hi, a_lo, b_hi, b_lo):
        dots = nt(a_hi, b_hi) + (nt(a_hi, b_lo) + nt(a_lo, b_hi))
        e = jnp.exp(dots * GAIN) * SHARE
        hi = e.astype(BF16)
        return hi, (e - hi.astype(F32)).astype(BF16)

    def build(t, first):
        at = lane_of(t)

        def body(r, _):
            acc = jnp.zeros((16, N), F32)
            for u in range(CAP):
                b, q = tabs_sm[r, u, at], tabs_sm[r, CAP + u, at]
                s = r * sb + jnp.maximum(b, 0)
                w = jnp.maximum(q, 0)
                hi, lo = tile(s_hi[s], s_lo[s], t_hi[t, w], t_lo[t, w])
                k_hi[r, t * CAP + u] = hi
                k_lo[r, t * CAP + u] = lo
                ones = jnp.where(sub16 == b, 1.0, 0.0).astype(BF16)
                acc = acc + nt(ones, hi) + nt(ones, lo)
            if first:
                rp0[r] = acc[:8]
            else:
                rp0[r] = rp0[r] + acc[:8]
            return 0

        lax.fori_loop(0, nr, body, 0)

    def far_tile(f, acc):
        w = tabf_sm[2 * CAP, f]
        hi, lo = tile(f_hi[f], f_lo[f], t_hi[0, w], t_lo[0, w])
        kf_hi[f] = hi
        kf_lo[f] = lo
        ones = jnp.where(sub16 == f, 1.0, 0.0).astype(BF16)
        return acc + nt(ones, hi) + nt(ones, lo)

    rf0[...] = lax.fori_loop(0, sb, far_tile, jnp.zeros((16, N), F32))[:8]
    build(0, True)
    build(NX - 1, False)
    build(1, False)
    for i in range(mid):
        relay_plus[i].wait_recv()
        norm_t(2, i * CHUNK, CHUNK)
        j = minus_order[i]
        relay_minus[j].wait_recv()
        norm_t(2, j * CHUNK, CHUNK)
    build(2, False)

    others = [(dz, flip) for dz in range(nz) for flip in range(2) if (dz, flip) != (0, 0)]
    across = range(1, NX)

    def spread(r, v, base):
        hi, lo = halves(v)
        return jnp.where(sub16 == r, hi, jnp.where(sub16 == r + base, lo, 0.0)).astype(BF16)

    def rows_pass(rp, rf):
        def body(r, _):
            acc = jnp.zeros((16, N), F32)
            for t in range(NX):
                at = lane_of(t)
                for u in range(CAP):
                    b, q = tabs_sm[r, u, at], tabs_sm[r, CAP + u, at]
                    lhs = spread(b, ts[t, pl.ds(jnp.maximum(q, 0), 1), :], 8)
                    acc = acc + nt(lhs, k_hi[r, t * CAP + u]) + nt(lhs, k_lo[r, t * CAP + u])
            rp[r] = acc[:8] + acc[8:]
            return 0

        lax.fori_loop(0, nr, body, 0)
        acc = jnp.zeros((16, N), F32)
        for f in range(sb):
            lhs = spread(f, ts[0, pl.ds(tabf_sm[2 * CAP, f], 1), :], 8)
            acc = acc + nt(lhs, kf_hi[f]) + nt(lhs, kf_lo[f])
        rf[...] = acc[:8] + acc[8:]

    def cols_pass(ss, sf):
        def one(v, hi, lo, q, acc):
            lhs = spread(0, v, 1)
            o = nn(lhs, hi) + nn(lhs, lo)
            return acc + jnp.where(sub32 == q, o[0:1] + o[1:2], 0.0)

        def body(r, accs):
            accs = list(accs)
            for t in range(NX):
                at = lane_of(t)
                for u in range(CAP):
                    b, q = tabs_sm[r, u, at], tabs_sm[r, CAP + u, at]
                    v = ss[r, pl.ds(jnp.maximum(b, 0), 1), :]
                    accs[t] = one(v, k_hi[r, t * CAP + u], k_lo[r, t * CAP + u], q, accs[t])
            return tuple(accs)

        zero = jnp.zeros((tb_dev, N), F32)
        accs = list(lax.fori_loop(0, nr, body, (zero,) * NX))
        for f in range(sb):
            accs[0] = one(sf[f : f + 1, :], kf_hi[f], kf_lo[f], tabf_sm[2 * CAP, f], accs[0])
        return accs

    for it, (rp, rpi, rf, rfi, so, ss, sf, co, ci) in enumerate((
        (rp0, rpi0, rf0, rfi0, so0, ss0, sf0, co0, ci0),
        (rp1, rpi1, rf1, rfi1, so1, ss1, sf1, co1, ci1),
    )):
        if it > 0:
            rows_pass(rp, rf)
        parts = [send(rf, rfi, behind)]
        for dz, flip in others:
            parts.append(send(rp.at[rel(dz, flip)], rpi.at[rel(-dz, flip)], dev(dz, 0, flip)))
        total = rp[0]
        for p in parts:
            p.wait_recv()
        total = total + rfi[...]
        for dz, flip in others:
            total = total + rpi[rel(dz, flip)]
        scale = smass[...] / (DUSTBIN + total)
        so[...] = scale
        ss[0] = scale
        if it == ITERS - 1:
            src_out[...] = scale
        parts = [send(so, sf, ahead)]
        for dz, flip in others:
            parts.append(send(so, ss.at[rel(-dz, flip)], dev(dz, 0, flip)))
        for p in parts:
            p.wait_recv()
        accs = cols_pass(ss, sf)
        parts = []
        for t in across:
            co[t] = accs[t]
        for t in across:
            parts.append(send(co.at[t], ci.at[NX - t], dev(0, t, 0)))
        total = accs[0]
        for p in parts:
            p.wait_recv()
        for t in across:
            total = total + ci[t]
        scale = tmass[...] / (DUSTBIN + total)
        if it == ITERS - 1:
            tgt_out[...] = scale
        else:
            to[...] = scale
            ts[0] = scale
            parts = [send(to, ts.at[NX - t], dev(0, t, 0)) for t in across]
            for p in parts:
                p.wait_recv()
    for copy in sent:
        copy.wait_send()


def local(ng, nz, semb, temb, smass, tmass, cdev, cblk):
    sb, tb = semb.shape[0], temb.shape[0]
    nr = 2 * nz
    near = NX * CAP
    vm = pltpu.VMEM
    tile = (N, N)
    scratch = [
        vm((nr, sb) + tile, F32), vm((NX, tb) + tile, F32), vm((sb,) + tile, F32),
        vm((nr * sb,) + tile, BF16), vm((nr * sb,) + tile, BF16),
        vm((NX, tb) + tile, BF16), vm((NX, tb) + tile, BF16),
        vm((sb,) + tile, BF16), vm((sb,) + tile, BF16),
        vm((nr, near) + tile, BF16), vm((nr, near) + tile, BF16),
        vm((sb,) + tile, BF16), vm((sb,) + tile, BF16),
        vm((8, N), I32), vm((nr, 8, N), I32), vm((8, N), I32),
        pltpu.SMEM((nr, 8, N), I32), pltpu.SMEM((8, N), I32),
    ]
    scratch += [vm((nr, sb, N), F32)] * 4 + [vm((sb, N), F32)] * 4 + [vm((sb, N), F32)] * 2
    scratch += [vm((nr, sb, N), F32)] * 2 + [vm((sb, N), F32)] * 2
    scratch += [vm((NX, tb, N), F32)] * 4 + [vm((tb, N), F32), vm((NX, tb, N), F32)]
    scratch += [pltpu.SemaphoreType.DMA((128,)), pltpu.SemaphoreType.DMA((128,)), pltpu.SemaphoreType.DMA((4,))]
    any_, vmem = pl.BlockSpec(memory_space=pl.ANY), pl.BlockSpec(memory_space=pltpu.VMEM)
    return pl.pallas_call(
        functools.partial(kernel, ng, nz, sb, tb),
        out_shape=(jax.ShapeDtypeStruct(smass.shape, F32), jax.ShapeDtypeStruct(tmass.shape, F32)),
        in_specs=[any_, any_, vmem, vmem, vmem, vmem],
        out_specs=(vmem, vmem),
        scratch_shapes=scratch,
        compiler_params=pltpu.CompilerParams(
            collective_id=0, has_side_effects=True, vmem_limit_bytes=60 * 1024 * 1024),
        name="sinkhorn",
    )(semb, temb, smass, tmass, cdev, cblk)


def solution(mesh):
    placed = (
        P(("group", "dev"), None, None),
        P(("group", "dev"), None, None),
        P(("group", "dev"), None),
        P(("group", "dev"), None),
        P(("group", "dev"), None),
        P(("group", "dev"), None),
    )
    ng, nz = mesh.shape["group"], mesh.shape["dev"] // (2 * NX)
    return jax.shard_map(
        functools.partial(local, ng, nz),
        mesh=mesh,
        in_specs=placed,
        out_specs=(P(("group", "dev"), None), P(("group", "dev"), None)),
        check_vma=False,
    )
```

time: 326 us -> 173 us (0.53)
  waiting for transfers between devices: 208 us -> 0 us
  Pallas kernels: 0 us -> 169 us
  starting transfers between devices: 55.7 us -> 0 us
  matrix products: 20.1 us -> 0 us
  local copies, waits for them, and re-layouts: 22 us -> 2.59 us
  other arithmetic: 18.1 us -> 0 us
    pallas_call x0 -> x1, Pallas kernels: none -> 169 us  [local(): pl.pallas_call(functools.partial(kernel, ng, nz, sb, tb), out_shape=(jax....]
    all_to_all x6 -> x0, waiting for transfers between devices: 158 us -> none  [the longest x1 133 us: local(): lax.all_to_all(selected_rows(tgt_unit, asked_rows, dev_count, slot_cap),...]
    ppermute x4 -> x0, waiting for transfers between devices: 50.1 us -> none  [from_behind(): return lax.ppermute(x, axis, [(i, (i + by) % count) for i in range(count)])]
    all_to_all x6 -> x0, starting transfers between devices: 48.2 us -> none  [the longest x2 14.5 us: local(): lax.all_to_all(departing_messages.reshape(dev_count, slot_cap, col_parts....]
    dot_general x9 -> x0, matrix products: 20.1 us -> none  [the longest x2 7.21 us: local(): jnp.einsum('ikbj,ib->ikj', kernel, src_scale, precision=lax.Precision.HIG...]
    gather x8 -> x0, local copies, waits for them, and re-layouts: 15.5 us -> none  [the longest x3 7.21 us: assemble(): jnp.take(nearby_flattened, slot_index, axis=0)]
    select_n x10 -> x0, other arithmetic: 11.3 us -> none  [the longest x4 8.64 us: selected_rows(): picked = jnp.take(table, asked_rows, axis=0)]
    ppermute x4 -> x0, starting transfers between devices: 7.48 us -> none  [from_behind(): return lax.ppermute(x, axis, [(i, (i + by) % count) for i in range(count)])]
  transfers between devices with their start and end apart: 10 -> 0, of which waited for: 8 -> 0; matrix products, arithmetic and copies ran while one was open for 7% -> 0% of each run, Pallas kernels for 0% -> 0%
where the time goes in v1:
time: 173 us; the launch traced here: 172 us
  Pallas kernels  169 us (98%)
  local copies, waits for them, and re-layouts  2.59 us (1%)
    pallas_call x1, Pallas kernels, local(): pl.pallas_call(functools.partial(kernel, ng, nz, sb, tb), out_shape=(jax....  169 us

profile of v1, /device:TPU:1, one launch (start us, length us, event | category | flops | bytes accessed | tf_op | source)
XLA Modules:
  0.0 172.2 jit_solution(17276786025964881798)
XLA Ops:
  0.6 169.0 %sinkhorn.1 = (f32[8,128]{1,0:T(8,128)}, f32[32,128]{1,0:T(8,128)}) custom-call(f32[8,128,128]{2,1,0:T(8,128)} %refs_0_.1, f32[32,128,128]{2,1,0:T(8,128)} %refs_1_.1, f32[8,128]{1,0:T(8,128)} %refs_2_.1, f32[32,128]{1,0:T(8,128)} %refs_3_.1, s32[8,7]{1,0:T(8,128)} %refs_4_.1, s32[8,8]{1,0:T(8,128)} %refs_5_.1), custom_call_target="tpu_custom_call" | custom-call | tf_op jit(solution)/shard_map/sinkhorn/pallas_call | solution.py:381
  169.6 1.3 copy.10
  170.9 1.3 copy.11

commit v2 on v1

v2 whole, which is shorter than its diff:
```python
import functools

import jax
import jax.numpy as jnp
from jax import lax
from jax.experimental import pallas as pl
from jax.experimental.pallas import tpu as pltpu
from jax.sharding import PartitionSpec as P

MESH = pl.DeviceIdType.MESH
N = 128
NX = 4
NEAR = 7
CAP = 2
ITERS = 2
EMPTY = -64
CHUNK = 8
DUSTBIN = 0.5
EPSILON = 1e-6
GAIN = 1.0 / (N * 0.1)
SHARE = 1.0 / (8.0 * N)

F32, BF16, I32 = jnp.float32, jnp.bfloat16, jnp.int32


def nn(a, b):
    return lax.dot_general(a, b, (((1,), (0,)), ((), ())), preferred_element_type=F32)


def halves(v):
    hi = v.astype(BF16).astype(F32)
    return hi, v - hi


def kernel(ng, nz, sb, tb_dev, *refs):
    (semb, temb, smass, tmass, cdev, cblk, src_out, tgt_out,
     s_raw, t_raw, f_raw, s_hi, s_lo, t_hi, t_lo, f_hi, f_lo, k_row, k_col, kf_row, kf_col,
     tab, tabs, tabf, tabc, tabs_sm, tabf_sm,
     rp0, rp1, rpi0, rpi1, rf0, rf1, rfi0, rfi1, so0, so1, ss0, ss1, sf0, sf1,
     co0, co1, ci0, ci1, to, ts, snd, rcv, loc) = refs
    nr = 2 * nz
    hops = nz // 2
    half = sb // 2
    line = 2 * NX
    g, d = lax.axis_index("group"), lax.axis_index("dev")
    z, x, c = d // line, (d // 2) % NX, d % 2

    def dev(dz, dx, flip):
        zz, xx = lax.rem(z + dz, nz), lax.rem(x + dx, NX)
        return (g, zz * line + xx * 2 + (1 - c if flip else c))

    def rel(dz, flip):
        return (dz % nz) * 2 + flip

    up, down = dev(1, 0, 0), dev(nz - 1, 0, 0)
    right, left = dev(0, 1, 0), dev(0, NX - 1, 0)
    partner = dev(0, 0, 1)
    ahead, behind = (lax.rem(g + 1, ng), d), (lax.rem(g + ng - 1, ng), d)

    count = [0]
    sent = []

    def send(src, dst, to_dev):
        k = count[0]
        count[0] += 1
        copy = pltpu.make_async_remote_copy(
            src_ref=src, dst_ref=dst, send_sem=snd.at[k], recv_sem=rcv.at[k],
            device_id=to_dev, device_id_type=MESH)
        copy.start()
        sent.append(copy)
        return copy

    barrier = pltpu.get_barrier_semaphore()
    greeted = (up, down, right, left, partner, ahead, behind)
    for other in greeted:
        pl.semaphore_signal(barrier, inc=1, device_id=other, device_id_type=MESH)
    own_s = pltpu.make_async_copy(semb, s_raw.at[0], loc.at[0])
    own_t = pltpu.make_async_copy(temb, t_raw.at[0], loc.at[1])
    own_s.start()
    own_t.start()

    lane = lax.broadcasted_iota(I32, (1, N), 1)
    run = jnp.zeros((1, N), I32)
    rows = [jnp.full((1, N), EMPTY, I32) for _ in range(2 * CAP)]
    far = jnp.zeros((1, N), I32)
    for b in range(sb):
        hit = jnp.zeros((1, N), I32)
        which = jnp.zeros((1, N), I32)
        for k in range(NEAR):
            m = cdev[b : b + 1, k : k + 1] == lane
            hit = jnp.where(m, 1, hit)
            which = jnp.where(m, cblk[b : b + 1, k : k + 1], which)
        for u in range(CAP):
            m = (hit == 1) & (run == u)
            rows[u] = jnp.where(m, b, rows[u])
            rows[CAP + u] = jnp.where(m, which, rows[CAP + u])
        run = run + hit
        far = jnp.where(lane == b, cblk[b : b + 1, NEAR : NEAR + 1], far)
    table = jnp.concatenate(rows + [far] + [jnp.zeros((1, N), I32)] * (7 - 2 * CAP), axis=0)
    tab[...] = table
    tabs[0] = table

    pl.semaphore_wait(barrier, len(greeted))

    chunks = tb_dev // CHUNK
    mid = chunks // 2
    minus_order = list(range(mid, chunks)) + list(range(mid))
    w_plus = {1: send(tab, tabs.at[rel(-1, 0)], up)}
    w_minus = {1: send(tab, tabs.at[rel(1, 0)], down)}
    s_plus = {1: send(semb, s_raw.at[rel(-1, 0)], up)}
    s_minus = {1: send(semb, s_raw.at[rel(1, 0)], down)}
    t_plus, t_minus = {}, {}
    for i in range(chunks):
        p, m = pl.ds(i * CHUNK, CHUNK), pl.ds(minus_order[i] * CHUNK, CHUNK)
        t_plus[i] = send(temb.at[p], t_raw.at[NX - 1, p], right)
        t_minus[minus_order[i]] = send(temb.at[m], t_raw.at[1, m], left)
    w_far = send(tab, tabf, ahead)
    f_far = send(semb, f_raw, ahead)
    w_mate = {0: send(tab, tabs.at[rel(0, 1)], partner)}
    s_mate = {0: send(semb, s_raw.at[rel(0, 1)], partner)}

    def normalize(raw, hi, lo, start, size, into, turned):
        def one(i, _):
            for w in range(8):
                k = i * 8 + w
                v = raw[start + k]
                if turned:
                    v = v.T
                axis = 0 if turned else 1
                v = v * lax.rsqrt(jnp.mean(v * v, axis=axis, keepdims=True) + EPSILON)
                h = v.astype(BF16)
                hi[into + k] = h
                lo[into + k] = (v - h.astype(F32)).astype(BF16)
            return 0

        lax.fori_loop(0, size // 8, one, 0)

    def norm_s(dz, flip):
        r = rel(dz, flip)
        normalize(s_raw.at[r], s_hi, s_lo, 0, sb, r * sb, True)

    def norm_t(t, start, size):
        normalize(t_raw.at[t], t_hi.at[t], t_lo.at[t], start, size, start, False)

    own_s.wait()
    norm_s(0, 0)
    own_t.wait()
    norm_t(0, 0, tb_dev)
    relay_plus, relay_minus = {}, {}
    for h in range(1, hops + 1):
        a, b = rel(-h, 0), rel(h, 0)
        w_plus[h].wait_recv()
        if h < hops:
            w_plus[h + 1] = send(tabs.at[a], tabs.at[rel(-h - 1, 0)], up)
        w_mate[-h] = send(tabs.at[a], tabs.at[rel(-h, 1)], partner)
        if h < hops:
            w_minus[h].wait_recv()
            if h + 1 < hops:
                w_minus[h + 1] = send(tabs.at[b], tabs.at[rel(h + 1, 0)], down)
            w_mate[h] = send(tabs.at[b], tabs.at[rel(h, 1)], partner)
        s_plus[h].wait_recv()
        s_minus[h].wait_recv()
        if h + 1 < hops:
            s_plus[h + 1] = send(s_raw.at[a], s_raw.at[rel(-h - 1, 0)], up)
            s_minus[h + 1] = send(s_raw.at[b], s_raw.at[rel(h + 1, 0)], down)
        elif h + 1 == hops:
            lo_half, hi_half = pl.ds(0, half), pl.ds(half, half)
            last = rel(hops, 0)
            s_plus[hops] = send(s_raw.at[a, lo_half], s_raw.at[last, lo_half], up)
            s_minus[hops] = send(s_raw.at[b, hi_half], s_raw.at[last, hi_half], down)
        s_mate[-h] = send(s_raw.at[a], s_raw.at[rel(-h, 1)], partner)
        if h < hops:
            s_mate[h] = send(s_raw.at[b], s_raw.at[rel(h, 1)], partner)
        if h <= chunks:
            i, j = h - 1, minus_order[h - 1]
            pi, pj = pl.ds(i * CHUNK, CHUNK), pl.ds(j * CHUNK, CHUNK)
            t_plus[i].wait_recv()
            if i < mid:
                relay_plus[i] = send(t_raw.at[NX - 1, pi], t_raw.at[2, pi], right)
            t_minus[j].wait_recv()
            if j >= mid:
                relay_minus[j] = send(t_raw.at[1, pj], t_raw.at[2, pj], left)
        norm_s(-h, 0)
        if h < hops:
            norm_s(h, 0)
        if h <= chunks:
            norm_t(NX - 1, i * CHUNK, CHUNK)
            norm_t(1, j * CHUNK, CHUNK)
    for copy in w_mate.values():
        copy.wait_recv()
    lane8 = lax.broadcasted_iota(I32, (8, N), 1)
    compact = jnp.zeros((8, N), I32)
    for r in range(nr):
        moved = pltpu.roll(tabs[r], lax.rem(r * line + N - z * line, N), 1)
        compact = jnp.where(lane8 // line == r, moved, compact)
    tabc[...] = compact
    w_far.wait_recv()
    far_table = pltpu.make_async_copy(tabf, tabf_sm, loc.at[3])
    far_table.start()
    f_far.wait_recv()
    normalize(f_raw, f_hi, f_lo, 0, sb, 0, True)
    tables = pltpu.make_async_copy(tabc, tabs_sm, loc.at[2])
    tables.start()
    for dz, copy in s_mate.items():
        copy.wait_recv()
        norm_s(dz, 1)
    far_table.wait()
    tables.wait()

    sub8 = lax.broadcasted_iota(I32, (8, N), 0)
    sub16 = lax.broadcasted_iota(I32, (16, N), 0)
    sub32 = lax.broadcasted_iota(I32, (tb_dev, N), 0)

    def lane_of(r, t):
        return r * line + lax.rem(x + t, NX) * 2 + c

    def two_terms(v, ref, k):
        hi = v.astype(BF16)
        ref[pl.ds(k * 2 * N, N), :] = hi
        ref[pl.ds(k * 2 * N + N, N), :] = (v - hi.astype(F32)).astype(BF16)

    def tile(b_hi, b_lo, a_hi, a_lo, row, col, k):
        dots = nn(b_hi, a_hi) + (nn(b_lo, a_hi) + nn(b_hi, a_lo))
        e = jnp.exp(dots * GAIN) * SHARE
        two_terms(e, row, k)
        two_terms(e.T, col, k)
        return jnp.sum(e, axis=0, keepdims=True)

    def build(t, first):
        def body(r0, _):
            for rr in range(4):
                r = r0 * 4 + rr
                acc = jnp.zeros((8, N), F32)
                for u in range(CAP):
                    b, q = tabs_sm[u, lane_of(r, t)], tabs_sm[CAP + u, lane_of(r, t)]
                    s = r * sb + jnp.maximum(b, 0)
                    w = jnp.maximum(q, 0)
                    sums = tile(t_hi[t, w], t_lo[t, w], s_hi[s], s_lo[s],
                                k_row.at[r], k_col.at[r], t * CAP + u)
                    acc = acc + jnp.where(sub8 == b, sums, 0.0)
                rp0[r] = acc if first else rp0[r] + acc
            return 0

        lax.fori_loop(0, nr // 4, body, 0)

    def far_tiles(f0, acc):
        for ff in range(4):
            f = f0 * 4 + ff
            w = tabf_sm[2 * CAP, f]
            sums = tile(t_hi[0, w], t_lo[0, w], f_hi[f], f_lo[f], kf_row, kf_col, f)
            acc = acc + jnp.where(sub8 == f, sums, 0.0)
        return acc

    rf0[...] = lax.fori_loop(0, sb // 4, far_tiles, jnp.zeros((8, N), F32))
    build(0, True)
    build(NX - 1, False)
    build(1, False)
    for i in range(mid):
        relay_plus[i].wait_recv()
        norm_t(2, i * CHUNK, CHUNK)
        j = minus_order[i]
        relay_minus[j].wait_recv()
        norm_t(2, j * CHUNK, CHUNK)
    build(2, False)

    others = [(dz, flip) for dz in range(nz) for flip in range(2) if (dz, flip) != (0, 0)]
    others.sort(key=lambda o: -min(o[0], nz - o[0]))
    across = (2, 1, 3)

    def spread(v, r):
        hi, lo = halves(v)
        return jnp.where(sub16 == r, hi, jnp.where(sub16 == r + 8, lo, 0.0)).astype(BF16)

    def product(lhs, tiles):
        o = nn(jnp.concatenate([v for v in lhs for _ in range(2)], axis=1), tiles)
        return o[:8] + o[8:]

    def rows_pass(rp, rf):
        def body(r0, _):
            for rr in range(4):
                r = r0 * 4 + rr
                lhs = []
                for t in range(NX):
                    for u in range(CAP):
                        b, q = tabs_sm[u, lane_of(r, t)], tabs_sm[CAP + u, lane_of(r, t)]
                        lhs.append(spread(ts[t, pl.ds(jnp.maximum(q, 0), 1), :], b))
                rp[r] = product(lhs, k_row[r])
            return 0

        lax.fori_loop(0, nr // 4, body, 0)
        lhs = [spread(ts[0, pl.ds(tabf_sm[2 * CAP, f], 1), :], f) for f in range(sb)]
        rf[...] = product(lhs, kf_row[...])

    def cols_pass(ss, sf):
        def body(r0, accs):
            accs = list(accs)
            for rr in range(4):
                r = r0 * 4 + rr
                lhs = []
                for t in range(NX):
                    for u in range(CAP):
                        b = tabs_sm[u, lane_of(r, t)]
                        lhs.append(spread(ss[r, pl.ds(jnp.maximum(b, 0), 1), :], t * CAP + u))
                o = product(lhs, k_col[r])
                for t in range(NX):
                    for u in range(CAP):
                        k = t * CAP + u
                        q = tabs_sm[CAP + u, lane_of(r, t)]
                        accs[t] = accs[t] + jnp.where(sub32 == q, o[k : k + 1], 0.0)
            return tuple(accs)

        lhs = [spread(sf[f : f + 1, :], f) for f in range(sb)]
        o = product(lhs, kf_col[...])
        first = jnp.zeros((tb_dev, N), F32)
        for f in range(sb):
            first = first + jnp.where(sub32 == tabf_sm[2 * CAP, f], o[f : f + 1], 0.0)
        zero = jnp.zeros((tb_dev, N), F32)
        return lax.fori_loop(0, nr // 4, body, (first, zero, zero, zero))

    for it, (rp, rpi, rf, rfi, so, ss, sf, co, ci) in enumerate((
        (rp0, rpi0, rf0, rfi0, so0, ss0, sf0, co0, ci0),
        (rp1, rpi1, rf1, rfi1, so1, ss1, sf1, co1, ci1),
    )):
        if it > 0:
            rows_pass(rp, rf)
        parts = []
        for dz, flip in others:
            parts.append(send(rp.at[rel(dz, flip)], rpi.at[rel(-dz, flip)], dev(dz, 0, flip)))
        parts.append(send(rf, rfi, behind))
        total = rp[0]
        for p in parts:
            p.wait_recv()
        total = total + rfi[...]
        for dz, flip in others:
            total = total + rpi[rel(dz, flip)]
        scale = smass[...] / (DUSTBIN + total)
        so[...] = scale
        ss[0] = scale
        if it == ITERS - 1:
            src_out[...] = scale
        parts = []
        for dz, flip in others:
            parts.append(send(so, ss.at[rel(-dz, flip)], dev(dz, 0, flip)))
        parts.append(send(so, sf, ahead))
        for p in parts:
            p.wait_recv()
        accs = cols_pass(ss, sf)
        parts = []
        for t in across:
            co[t] = accs[t]
        for t in across:
            parts.append(send(co.at[t], ci.at[NX - t], dev(0, t, 0)))
        total = accs[0]
        for p in parts:
            p.wait_recv()
        for t in across:
            total = total + ci[t]
        scale = tmass[...] / (DUSTBIN + total)
        if it == ITERS - 1:
            tgt_out[...] = scale
        else:
            to[...] = scale
            ts[0] = scale
            parts = [send(to, ts.at[NX - t], dev(0, t, 0)) for t in across]
            for p in parts:
                p.wait_recv()
    for copy in sent:
        copy.wait_send()


def local(ng, nz, semb, temb, smass, tmass, cdev, cblk):
    sb, tb = semb.shape[0], temb.shape[0]
    nr = 2 * nz
    slots = NX * CAP * 2 * N
    vm = pltpu.VMEM
    tile = (N, N)
    scratch = [
        vm((nr, sb) + tile, F32), vm((NX, tb) + tile, F32), vm((sb,) + tile, F32),
        vm((nr * sb,) + tile, BF16), vm((nr * sb,) + tile, BF16),
        vm((NX, tb) + tile, BF16), vm((NX, tb) + tile, BF16),
        vm((sb,) + tile, BF16), vm((sb,) + tile, BF16),
        vm((nr, slots, N), BF16), vm((nr, slots, N), BF16),
        vm((sb * 2 * N, N), BF16), vm((sb * 2 * N, N), BF16),
        vm((8, N), I32), vm((nr, 8, N), I32), vm((8, N), I32), vm((8, N), I32),
        pltpu.SMEM((8, N), I32), pltpu.SMEM((8, N), I32),
    ]
    scratch += [vm((nr, sb, N), F32)] * 4 + [vm((sb, N), F32)] * 4 + [vm((sb, N), F32)] * 2
    scratch += [vm((nr, sb, N), F32)] * 2 + [vm((sb, N), F32)] * 2
    scratch += [vm((NX, tb, N), F32)] * 4 + [vm((tb, N), F32), vm((NX, tb, N), F32)]
    scratch += [pltpu.SemaphoreType.DMA((128,)), pltpu.SemaphoreType.DMA((128,)), pltpu.SemaphoreType.DMA((4,))]
    any_, vmem = pl.BlockSpec(memory_space=pl.ANY), pl.BlockSpec(memory_space=pltpu.VMEM)
    return pl.pallas_call(
        functools.partial(kernel, ng, nz, sb, tb),
        out_shape=(jax.ShapeDtypeStruct(smass.shape, F32), jax.ShapeDtypeStruct(tmass.shape, F32)),
        in_specs=[any_, any_, vmem, vmem, vmem, vmem],
        out_specs=(vmem, vmem),
        scratch_shapes=scratch,
        compiler_params=pltpu.CompilerParams(
            collective_id=0, has_side_effects=True, vmem_limit_bytes=60 * 1024 * 1024),
        name="sinkhorn",
    )(semb, temb, smass, tmass, cdev, cblk)


def solution(mesh):
    placed = (
        P(("group", "dev"), None, None),
        P(("group", "dev"), None, None),
        P(("group", "dev"), None),
        P(("group", "dev"), None),
        P(("group", "dev"), None),
        P(("group", "dev"), None),
    )
    ng, nz = mesh.shape["group"], mesh.shape["dev"] // (2 * NX)
    return jax.shard_map(
        functools.partial(local, ng, nz),
        mesh=mesh,
        in_specs=placed,
        out_specs=(P(("group", "dev"), None), P(("group", "dev"), None)),
        check_vma=False,
    )
```

time: 173 us -> 122 us (0.71)
  Pallas kernels: 169 us -> 119 us
    pallas_call x1, Pallas kernels: 169 us -> 119 us  [local(): pl.pallas_call(functools.partial(kernel, ng, nz, sb, tb), out_shape=(jax....]
where the time goes in v2:
time: 122 us
  Pallas kernels  119 us (98%)
  local copies, waits for them, and re-layouts  2.59 us (2%)
    pallas_call x1, Pallas kernels, local(): pl.pallas_call(functools.partial(kernel, ng, nz, sb, tb), out_shape=(jax....  119 us
    unnamed x2, local copies, waits for them, and re-layouts  2.59 us

profile of v2, /device:TPU:1, one launch (start us, length us, event | category | flops | bytes accessed | tf_op | source)
XLA Modules:
  0.0 121.8 jit_solution(15681192267744620143)
XLA Ops:
  0.6 118.6 %sinkhorn.1 = (f32[8,128]{1,0:T(8,128)}, f32[32,128]{1,0:T(8,128)}) custom-call(f32[8,128,128]{2,1,0:T(8,128)} %refs_0_.1, f32[32,128,128]{2,1,0:T(8,128)} %refs_1_.1, f32[8,128]{1,0:T(8,128)} %refs_2_.1, f32[32,128]{1,0:T(8,128)} %refs_3_.1, s32[8,7]{1,0:T(8,128)} %refs_4_.1, s32[8,8]{1,0:T(8,128)} %refs_5_.1), custom_call_target="tpu_custom_call" | custom-call | tf_op jit(solution)/shard_map/sinkhorn/pallas_call | solution.py:392
  119.2 1.3 %copy.10 = f32[8,128]{1,0:T(8,128)} copy(f32[8,128]{1,0:T(8,128)} %get-tuple-element.4) | data formatting | bytes 8192
  120.5 1.3 %copy.11 = f32[32,128]{1,0:T(8,128)} copy(f32[32,128]{1,0:T(8,128)} %get-tuple-element.5) | data formatting | bytes 32768

commit v3 on v2

--- a/solution.py
+++ b/solution.py
@@ -15,6 +15,7 @@
 ITERS = 2
 EMPTY = -64
 CHUNK = 8
+COPIES = 45
 DUSTBIN = 0.5
 EPSILON = 1e-6
 GAIN = 1.0 / (N * 0.1)
@@ -33,11 +34,12 @@
 
 
 def kernel(ng, nz, sb, tb_dev, *refs):
-    (semb, temb, smass, tmass, cdev, cblk, src_out, tgt_out,
+    (semb, temb, smass_in, tmass_in, cdev_in, cblk_in, out,
      s_raw, t_raw, f_raw, s_hi, s_lo, t_hi, t_lo, f_hi, f_lo, k_row, k_col, kf_row, kf_col,
      tab, tabs, tabf, tabc, tabs_sm, tabf_sm,
-     rp0, rp1, rpi0, rpi1, rf0, rf1, rfi0, rfi1, so0, so1, ss0, ss1, sf0, sf1,
-     co0, co1, ci0, ci1, to, ts, snd, rcv, loc) = refs
+     rp0, rp1, rpi0, rpi1, rf0, rf1, rfi0, rfi1, so0, so1, ss0, ss1, ssl, sf0, sf1,
+     co0, co1, ci0, ci1, to, ts, smass, tmass, cdev, cblk,
+     snd, rcv, rs_snd, rs_rcv, ag_snd, ag_rcv, ex_snd, ex_rcv, loc) = refs
     nr = 2 * nz
     hops = nz // 2
     half = sb // 2
@@ -76,8 +78,14 @@
         pl.semaphore_signal(barrier, inc=1, device_id=other, device_id_type=MESH)
     own_s = pltpu.make_async_copy(semb, s_raw.at[0], loc.at[0])
     own_t = pltpu.make_async_copy(temb, t_raw.at[0], loc.at[1])
+    small = [pltpu.make_async_copy(a, b, loc.at[4 + i]) for i, (a, b) in enumerate(
+        ((cdev_in, cdev), (cblk_in, cblk), (smass_in, smass), (tmass_in, tmass)))]
+    for copy in small:
+        copy.start()
     own_s.start()
     own_t.start()
+    for copy in small:
+        copy.wait()
 
     lane = lax.broadcasted_iota(I32, (1, N), 1)
     run = jnp.zeros((1, N), I32)
@@ -226,10 +234,35 @@
         two_terms(e.T, col, k)
         return jnp.sum(e, axis=0, keepdims=True)
 
-    def build(t, first):
+    def group(j):
+        near, far = lax.rem(nz - j, nz), j + 1
+        return (near, 0), (near, 1), (far, 0), (far, 1)
+
+    def to_line(src, dst, snds, rcvs, dz, flip, whole=False):
+        r, back = dz * 2 + flip, lax.rem(nz - dz, nz) * 2 + flip
+        return pltpu.make_async_remote_copy(
+            src_ref=src if whole else src.at[r], dst_ref=dst.at[back], send_sem=snds.at[r],
+            recv_sem=rcvs.at[back], device_id=dev(dz, 0, flip), device_id_type=MESH)
+
+    def from_line(src, dst, snds, rcvs, dz, flip, whole=False):
+        r = dz * 2 + flip
+        return pltpu.make_async_remote_copy(
+            src_ref=src if whole else src.at[r], dst_ref=dst.at[r], send_sem=snds.at[r],
+            recv_sem=rcvs.at[r], device_id=dev(dz, 0, flip), device_id_type=MESH)
+
+    def send_rows(rp, rpi, j):
+        for i, (dz, flip) in enumerate(group(j)):
+            copy = to_line(rp, rpi, rs_snd, rs_rcv, dz, flip)
+            if i == 0:
+                pl.when(j > 0)(copy.start)
+            else:
+                copy.start()
+
+    def build(t, first, last=False):
         def body(r0, _):
-            for rr in range(4):
-                r = r0 * 4 + rr
+            j = nz // 2 - 1 - r0
+            for dz, flip in group(j):
+                r = dz * 2 + flip
                 acc = jnp.zeros((8, N), F32)
                 for u in range(CAP):
                     b, q = tabs_sm[u, lane_of(r, t)], tabs_sm[CAP + u, lane_of(r, t)]
@@ -239,6 +272,8 @@
                                 k_row.at[r], k_col.at[r], t * CAP + u)
                     acc = acc + jnp.where(sub8 == b, sums, 0.0)
                 rp0[r] = acc if first else rp0[r] + acc
+            if last:
+                send_rows(rp0, rpi0, j)
             return 0
 
         lax.fori_loop(0, nr // 4, body, 0)
@@ -261,12 +296,17 @@
         j = minus_order[i]
         relay_minus[j].wait_recv()
         norm_t(2, j * CHUNK, CHUNK)
-    build(2, False)
+    build(2, False, True)
 
     others = [(dz, flip) for dz in range(nz) for flip in range(2) if (dz, flip) != (0, 0)]
     others.sort(key=lambda o: -min(o[0], nz - o[0]))
     across = (2, 1, 3)
 
+    def exchange(src, dst, k, to_dev):
+        return pltpu.make_async_remote_copy(
+            src_ref=src, dst_ref=dst, send_sem=ex_snd.at[k], recv_sem=ex_rcv.at[k],
+            device_id=to_dev, device_id_type=MESH)
+
     def spread(v, r):
         hi, lo = halves(v)
         return jnp.where(sub16 == r, hi, jnp.where(sub16 == r + 8, lo, 0.0)).astype(BF16)
@@ -275,32 +315,42 @@
         o = nn(jnp.concatenate([v for v in lhs for _ in range(2)], axis=1), tiles)
         return o[:8] + o[8:]
 
-    def rows_pass(rp, rf):
+    def rows_pass(rp, rpi, rf):
         def body(r0, _):
-            for rr in range(4):
-                r = r0 * 4 + rr
+            j = nz // 2 - 1 - r0
+            for dz, flip in group(j):
+                r = dz * 2 + flip
                 lhs = []
                 for t in range(NX):
                     for u in range(CAP):
                         b, q = tabs_sm[u, lane_of(r, t)], tabs_sm[CAP + u, lane_of(r, t)]
                         lhs.append(spread(ts[t, pl.ds(jnp.maximum(q, 0), 1), :], b))
                 rp[r] = product(lhs, k_row[r])
+            send_rows(rp, rpi, j)
             return 0
 
-        lax.fori_loop(0, nr // 4, body, 0)
+        lax.fori_loop(0, nz // 2, body, 0)
         lhs = [spread(ts[0, pl.ds(tabf_sm[2 * CAP, f], 1), :], f) for f in range(sb)]
         rf[...] = product(lhs, kf_row[...])
 
-    def cols_pass(ss, sf):
-        def body(r0, accs):
+    def cols_pass(so, ss, sf, far_copy):
+        def body(j, accs):
             accs = list(accs)
-            for rr in range(4):
-                r = r0 * 4 + rr
+            for i, (dz, flip) in enumerate(group(j)):
+                copy = from_line(so, ss, ag_snd, ag_rcv, dz, flip, True)
+                if i == 0:
+                    pl.when(j > 0)(copy.wait_recv)
+                else:
+                    copy.wait_recv()
+            for dz, flip in group(j):
+                ssl[dz * 2 + flip] = ss[dz * 2 + flip]
+            for dz, flip in group(j):
+                r = dz * 2 + flip
                 lhs = []
                 for t in range(NX):
                     for u in range(CAP):
                         b = tabs_sm[u, lane_of(r, t)]
-                        lhs.append(spread(ss[r, pl.ds(jnp.maximum(b, 0), 1), :], t * CAP + u))
+                        lhs.append(spread(ssl[r, pl.ds(jnp.maximum(b, 0), 1), :], t * CAP + u))
                 o = product(lhs, k_col[r])
                 for t in range(NX):
                     for u in range(CAP):
@@ -309,63 +359,76 @@
                         accs[t] = accs[t] + jnp.where(sub32 == q, o[k : k + 1], 0.0)
             return tuple(accs)
 
+        zero = jnp.zeros((tb_dev, N), F32)
+        accs = list(lax.fori_loop(0, nz // 2, body, (zero,) * NX))
+        far_copy.wait_recv()
         lhs = [spread(sf[f : f + 1, :], f) for f in range(sb)]
         o = product(lhs, kf_col[...])
-        first = jnp.zeros((tb_dev, N), F32)
         for f in range(sb):
-            first = first + jnp.where(sub32 == tabf_sm[2 * CAP, f], o[f : f + 1], 0.0)
-        zero = jnp.zeros((tb_dev, N), F32)
-        return lax.fori_loop(0, nr // 4, body, (first, zero, zero, zero))
+            accs[0] = accs[0] + jnp.where(sub32 == tabf_sm[2 * CAP, f], o[f : f + 1], 0.0)
+        return accs
 
     for it, (rp, rpi, rf, rfi, so, ss, sf, co, ci) in enumerate((
         (rp0, rpi0, rf0, rfi0, so0, ss0, sf0, co0, ci0),
         (rp1, rpi1, rf1, rfi1, so1, ss1, sf1, co1, ci1),
     )):
+        last = it == ITERS - 1
+        far_rows = exchange(rf, rfi, 0, behind)
+        far_scale = exchange(so, sf, 1, ahead)
         if it > 0:
-            rows_pass(rp, rf)
-        parts = []
-        for dz, flip in others:
-            parts.append(send(rp.at[rel(dz, flip)], rpi.at[rel(-dz, flip)], dev(dz, 0, flip)))
-        parts.append(send(rf, rfi, behind))
+            rows_pass(rp, rpi, rf)
+        far_rows.start()
         total = rp[0]
-        for p in parts:
-            p.wait_recv()
+        for dz, flip in others[::-1]:
+            from_line(rp, rpi, rs_snd, rs_rcv, dz, flip).wait_recv()
+        far_rows.wait_recv()
         total = total + rfi[...]
         for dz, flip in others:
             total = total + rpi[rel(dz, flip)]
         scale = smass[...] / (DUSTBIN + total)
         so[...] = scale
         ss[0] = scale
-        if it == ITERS - 1:
-            src_out[...] = scale
-        parts = []
+        if last:
+            out[:sb] = scale
         for dz, flip in others:
-            parts.append(send(so, ss.at[rel(-dz, flip)], dev(dz, 0, flip)))
-        parts.append(send(so, sf, ahead))
-        for p in parts:
-            p.wait_recv()
-        accs = cols_pass(ss, sf)
+            to_line(so, ss, ag_snd, ag_rcv, dz, flip, True).start()
+        far_scale.start()
+        accs = cols_pass(so, ss, sf, far_scale)
         parts = []
         for t in across:
             co[t] = accs[t]
         for t in across:
-            parts.append(send(co.at[t], ci.at[NX - t], dev(0, t, 0)))
+            copy = exchange(co.at[t], ci.at[NX - t], 1 + t, dev(0, t, 0))
+            copy.start()
+            parts.append(copy)
         total = accs[0]
+        for dz, flip in others:
+            to_line(rp, rpi, rs_snd, rs_rcv, dz, flip).wait_send()
+            to_line(so, ss, ag_snd, ag_rcv, dz, flip, True).wait_send()
+        far_rows.wait_send()
+        far_scale.wait_send()
         for p in parts:
             p.wait_recv()
         for t in across:
             total = total + ci[t]
         scale = tmass[...] / (DUSTBIN + total)
-        if it == ITERS - 1:
-            tgt_out[...] = scale
+        if last:
+            out[sb:] = scale
         else:
             to[...] = scale
             ts[0] = scale
-            parts = [send(to, ts.at[NX - t], dev(0, t, 0)) for t in across]
-            for p in parts:
+            spreads = [exchange(to, ts.at[NX - t], 4 + t, dev(0, t, 0)) for t in across]
+            for p in spreads:
+                p.start()
+            for p in spreads:
                 p.wait_recv()
+            for p in spreads:
+                p.wait_send()
+        for p in parts:
+            p.wait_send()
     for copy in sent:
         copy.wait_send()
+    assert count[0] <= COPIES
 
 
 def local(ng, nz, semb, temb, smass, tmass, cdev, cblk):
@@ -385,20 +448,34 @@
         pltpu.SMEM((8, N), I32), pltpu.SMEM((8, N), I32),
     ]
     scratch += [vm((nr, sb, N), F32)] * 4 + [vm((sb, N), F32)] * 4 + [vm((sb, N), F32)] * 2
-    scratch += [vm((nr, sb, N), F32)] * 2 + [vm((sb, N), F32)] * 2
+    scratch += [vm((nr, sb, N), F32)] * 3 + [vm((sb, N), F32)] * 2
     scratch += [vm((NX, tb, N), F32)] * 4 + [vm((tb, N), F32), vm((NX, tb, N), F32)]
-    scratch += [pltpu.SemaphoreType.DMA((128,)), pltpu.SemaphoreType.DMA((128,)), pltpu.SemaphoreType.DMA((4,))]
+    scratch += [vm(a.shape, a.dtype) for a in (smass, tmass, cdev, cblk)]
+    dma = pltpu.SemaphoreType.DMA
+    scratch += [dma((COPIES,))] * 2 + [dma((nr,))] * 4 + [dma((8,))] * 3
     any_, vmem = pl.BlockSpec(memory_space=pl.ANY), pl.BlockSpec(memory_space=pltpu.VMEM)
-    return pl.pallas_call(
+    both = pl.pallas_call(
         functools.partial(kernel, ng, nz, sb, tb),
-        out_shape=(jax.ShapeDtypeStruct(smass.shape, F32), jax.ShapeDtypeStruct(tmass.shape, F32)),
-        in_specs=[any_, any_, vmem, vmem, vmem, vmem],
-        out_specs=(vmem, vmem),
+        out_shape=jax.ShapeDtypeStruct((sb + tb, N), F32),
+        in_specs=[any_] * 6,
+        out_specs=vmem,
         scratch_shapes=scratch,
         compiler_params=pltpu.CompilerParams(
             collective_id=0, has_side_effects=True, vmem_limit_bytes=60 * 1024 * 1024),
         name="sinkhorn",
     )(semb, temb, smass, tmass, cdev, cblk)
+
+    def split(both_ref, src_ref, tgt_ref):
+        src_ref[...] = both_ref[:sb]
+        tgt_ref[...] = both_ref[sb:]
+
+    return pl.pallas_call(
+        split,
+        out_shape=(jax.ShapeDtypeStruct(smass.shape, F32), jax.ShapeDtypeStruct(tmass.shape, F32)),
+        in_specs=[vmem],
+        out_specs=(vmem, vmem),
+        name="split",
+    )(both)
 
 
 def solution(mesh):

time: 122 us -> 114 us (0.934)
  Pallas kernels: 119 us -> 114 us
  local copies, waits for them, and re-layouts: 2.59 us -> 0 us
    pallas_call x1 -> x2, Pallas kernels: 119 us -> 114 us  [the longest x1 112 us: local(): pl.pallas_call(functools.partial(kernel, ng, nz, sb, tb), out_shape=jax.S...]
    unnamed x2 -> x0, local copies, waits for them, and re-layouts: 2.59 us -> none
where the time goes in v3:
time: 114 us
  Pallas kernels  114 us (100%)
    pallas_call x1, Pallas kernels, local(): pl.pallas_call(functools.partial(kernel, ng, nz, sb, tb), out_shape=jax.S...  112 us

profile of v3, /device:TPU:1, one launch (start us, length us, event | category | flops | bytes accessed | tf_op | source)
XLA Modules:
  0.0 114.2 jit_solution(9477560116469237814)
XLA Ops:
  0.6 112.2 %sinkhorn.1.both_ref = f32[40,128]{1,0:T(8,128)} custom-call(f32[8,128,128]{2,1,0:T(8,128)} %refs_0_.1, f32[32,128,128]{2,1,0:T(8,128)} %refs_1_.1, f32[8,128]{1,0:T(8,128)} %refs_2_.1, f32[32,128]{1,0:T(8,128)} %refs_3_.1, s32[8,7]{1,0:T(8,128)} %refs_4_.1, s32[8,8]{1,0:T(8,128)} %refs_5_.1), custom_call_target="tpu_custom_call" | custom-call | tf_op jit(solution)/shard_map/sinkhorn/pallas_call | solution.py:457
  112.8 1.3 %split.1 = (f32[8,128]{1,0:T(8,128)}, f32[32,128]{1,0:T(8,128)}) custom-call(f32[40,128]{1,0:T(8,128)} %sinkhorn.1.both_ref), custom_call_target="tpu_custom_call" | custom-call | tf_op jit(solution)/shard_map/split/pallas_call | solution.py:472

commit v4 on v3

v4 whole, which is shorter than its diff:
```python
import functools

import jax
import jax.numpy as jnp
from jax import lax
from jax.experimental import pallas as pl
from jax.experimental.pallas import tpu as pltpu
from jax.sharding import PartitionSpec as P

MESH = pl.DeviceIdType.MESH
N = 128
NX = 4
NEAR = 7
CAP = 2
PAIR = 2
VMEM_BYTES = 62 * 1024 * 1024
ITERS = 2
EMPTY = -64
COPIES = 84
DUSTBIN = 0.5
EPSILON = 1e-6
GAIN = 1.0 / (N * 0.1)
SHARE = 1.0 / (8.0 * N)

F32, BF16, I32 = jnp.float32, jnp.bfloat16, jnp.int32


def nn(a, b):
    return lax.dot_general(a, b, (((1,), (0,)), ((), ())), preferred_element_type=F32)


def halves(v):
    hi = v.astype(BF16).astype(F32)
    return hi, v - hi


def kernel(ng, nz, sb, tb_dev, *refs):
    (semb, temb, smass_in, tmass_in, cdev_in, cblk_in, out,
     s_raw, t_raw, f_raw, s_hi, s_lo, t_hi, t_lo, f_hi, f_lo, k_row, k_col, kf_row, kf_col,
     tab, tabs, tabf, tabc, tabs_sm, tabf_sm,
     rp0, rp1, rpi0, rpi1, ss0, ss1, ssl, rf0, rf1, rfi0, rfi1, so0, so1, sf0, sf1,
     co0, co1, ci0, ci1, ts, smass, tmass, cdev, cblk, tmass_pair,
     snd, rcv, rs_snd, rs_rcv, ag_snd, ag_rcv, ex_snd, ex_rcv, loc) = refs
    nr = 4 * nz
    hops = nz // 2
    half = sb // 2
    quarter = sb // 4
    line = 2 * NX
    near = PAIR * CAP
    g, d = lax.axis_index("group"), lax.axis_index("dev")
    z, x, c = d // line, (d // 2) % NX, d % 2

    def at(zz, xx, cc):
        return (g, zz * line + xx * 2 + cc)

    def dev(dz, flip, bx):
        return at(lax.rem(z + dz, nz), NX - 1 - x if bx else x, 1 - c if flip else c)

    def rel(dz, flip, bx):
        return (dz % nz) * 4 + flip * 2 + bx

    up, down = dev(1, 0, 0), dev(nz - 1, 0, 0)
    partner, mate = dev(0, 1, 0), dev(0, 0, 1)
    pair = at(z, x + 1 - 2 * lax.rem(x, 2), c)
    ahead, behind = (lax.rem(g + 1, ng), d), (lax.rem(g + ng - 1, ng), d)

    count = [0]
    sent = []

    def send(src, dst, to_dev):
        k = count[0]
        count[0] += 1
        copy = pltpu.make_async_remote_copy(
            src_ref=src, dst_ref=dst, send_sem=snd.at[k], recv_sem=rcv.at[k],
            device_id=to_dev, device_id_type=MESH)
        copy.start()
        sent.append(copy)
        return copy

    barrier = pltpu.get_barrier_semaphore()
    greeted = (up, down, mate, pair, partner, ahead, behind)
    for other in greeted:
        pl.semaphore_signal(barrier, inc=1, device_id=other, device_id_type=MESH)
    own_s = pltpu.make_async_copy(semb, s_raw.at[0], loc.at[0])
    own_t = pltpu.make_async_copy(temb, t_raw.at[0], loc.at[1])
    small = [pltpu.make_async_copy(a, b, loc.at[4 + i]) for i, (a, b) in enumerate(
        ((cdev_in, cdev), (cblk_in, cblk), (smass_in, smass), (tmass_in, tmass)))]
    for copy in small:
        copy.start()
    own_s.start()
    own_t.start()
    for copy in small:
        copy.wait()

    lane = lax.broadcasted_iota(I32, (1, N), 1)
    run = jnp.zeros((1, N), I32)
    rows = [jnp.full((1, N), EMPTY, I32) for _ in range(2 * CAP)]
    far = jnp.zeros((1, N), I32)
    for b in range(sb):
        hit = jnp.zeros((1, N), I32)
        which = jnp.zeros((1, N), I32)
        for k in range(NEAR):
            m = cdev[b : b + 1, k : k + 1] == lane
            hit = jnp.where(m, 1, hit)
            which = jnp.where(m, cblk[b : b + 1, k : k + 1], which)
        for u in range(CAP):
            m = (hit == 1) & (run == u)
            rows[u] = jnp.where(m, b, rows[u])
            rows[CAP + u] = jnp.where(m, which, rows[CAP + u])
        run = run + hit
        far = jnp.where(lane == b, cblk[b : b + 1, NEAR : NEAR + 1], far)
    table = jnp.concatenate(rows + [far] + [jnp.zeros((1, N), I32)] * (7 - 2 * CAP), axis=0)
    tab[...] = table
    tabs[0] = table

    pl.semaphore_wait(barrier, len(greeted))

    lo, hi = pl.ds(0, half), pl.ds(half, half)
    pieces = ((0, half), (0, 0), (1, 0))
    z_plus, z_minus = {}, {}

    def piece(dz, p, start=0, size=half):
        bx, first = pieces[p]
        return s_raw.at[rel(dz, 0, bx), pl.ds(first + start, size)]

    w_mate = send(tab, tabs.at[1], mate)
    pre = send(semb.at[lo], s_raw.at[rel(0, 0, 1), lo], mate)
    for p in (0, 1):
        part = semb.at[pl.ds(pieces[p][1], half)]
        z_plus[1, p] = send(part, piece(-1, p), up)
        z_minus[1, p] = send(part, piece(1, p), down)
    post = {0: send(semb.at[hi], s_raw.at[rel(0, 0, 1), hi], mate)}
    t_pair = send(temb, t_raw.at[1], pair)
    mass_pair = send(tmass_in, tmass_pair, pair)
    cores = {0: [send(semb, s_raw.at[rel(0, 1, 0)], partner)]}
    w_far = send(tab, tabf, ahead)
    f_far = send(semb, f_raw, ahead)
    w_plus, w_minus, w_core = {}, {}, {}

    def two(dz, flip):
        return tabs.at[pl.ds(rel(dz, flip, 0), 2)]

    def unit(v, turned):
        if turned:
            v = v.T
        v = v * lax.rsqrt(jnp.mean(v * v, axis=0 if turned else 1, keepdims=True) + EPSILON)
        h = v.astype(BF16)
        return h, (v - h.astype(F32)).astype(BF16)

    def norm_lines(dz):
        def one(i, _):
            r = rel(dz, 0, 0) + i
            for w in range(sb):
                s_hi[r * sb + w], s_lo[r * sb + w] = unit(s_raw[r, w], True)
            return 0

        lax.fori_loop(0, 4, one, 0)

    def norm_t(t):
        def one(i, _):
            for w in range(8):
                t_hi[t, i * 8 + w], t_lo[t, i * 8 + w] = unit(t_raw[t, i * 8 + w], False)
            return 0

        lax.fori_loop(0, tb_dev // 8, one, 0)

    w_mate.wait_recv()
    w_plus[1] = send(two(0, 0), two(-1, 0), up)
    w_minus[1] = send(two(0, 0), two(1, 0), down)
    w_core[0] = send(two(0, 0), two(0, 1), partner)
    pre.wait_recv()
    z_plus[1, 2] = send(piece(0, 2), piece(-1, 2), up)
    z_minus[1, 2] = send(piece(0, 2), piece(1, 2), down)
    cores[0].append(send(piece(0, 2), s_raw.at[rel(0, 1, 1), lo], partner))
    own_t.wait()
    norm_t(0)
    own_s.wait()
    post[0].wait_recv()
    cores[0].append(send(s_raw.at[rel(0, 0, 1), hi], s_raw.at[rel(0, 1, 1), hi], partner))

    sub8 = lax.broadcasted_iota(I32, (8, N), 0)
    sub16 = lax.broadcasted_iota(I32, (16, N), 0)
    sub32 = lax.broadcasted_iota(I32, (tb_dev, N), 0)

    def lane_of(r, t):
        return r * 4 + lax.rem(x + t, 2) * 2 + c

    def two_terms(v, ref, k):
        h = v.astype(BF16)
        ref[pl.ds(k * 2 * N, N), :] = h
        ref[pl.ds(k * 2 * N + N, N), :] = (v - h.astype(F32)).astype(BF16)

    def tile(b_hi, b_lo, a_hi, a_lo, row, col, k):
        dots = nn(b_hi, a_hi) + (nn(b_lo, a_hi) + nn(b_hi, a_lo))
        e = jnp.exp(dots * GAIN) * SHARE
        two_terms(e, row, k)
        two_terms(e.T, col, k)
        return jnp.sum(e, axis=0, keepdims=True)

    def to_line(src, dst, snds, rcvs, dz, flip, bx, whole=False):
        r = dz * 4 + flip * 2 + bx
        back = lax.rem(nz - dz, nz) * 4 + flip * 2 + bx
        return pltpu.make_async_remote_copy(
            src_ref=src if whole else src.at[r], dst_ref=dst.at[back], send_sem=snds.at[r],
            recv_sem=rcvs.at[back], device_id=dev(dz, flip, bx), device_id_type=MESH)

    def from_line(src, dst, snds, rcvs, dz, flip, bx, whole=False):
        r = dz * 4 + flip * 2 + bx
        return pltpu.make_async_remote_copy(
            src_ref=src if whole else src.at[r], dst_ref=dst.at[r], send_sem=snds.at[r],
            recv_sem=rcvs.at[r], device_id=dev(dz, flip, bx), device_id_type=MESH)

    four = tuple((flip, bx) for flip in range(2) for bx in range(2))

    def send_rows(rp, rpi, dz):
        for flip, bx in four:
            copy = to_line(rp, rpi, rs_snd, rs_rcv, dz, flip, bx)
            if (flip, bx) == (0, 0):
                pl.when(dz > 0)(copy.start)
            else:
                copy.start()

    def build(dz):
        for flip in range(2):
            for bx in range(2):
                r = dz * 4 + flip * 2 + bx
                acc = jnp.zeros((8, N), F32)
                for t in range(PAIR):
                    for u in range(CAP):
                        b, q = tabs_sm[u, lane_of(r, t)], tabs_sm[CAP + u, lane_of(r, t)]
                        s, w = r * sb + jnp.maximum(b, 0), jnp.maximum(q, 0)
                        sums = tile(t_hi[t, w], t_lo[t, w], s_hi[s], s_lo[s], k_row.at[dz * 2 + flip],
                                    k_col.at[dz * 2 + flip], bx * near + t * CAP + u)
                        acc = acc + jnp.where(sub8 == b, sums, 0.0)
                rp0[r] = acc
        send_rows(rp0, rpi0, dz)

    def far_tiles(f0, acc):
        for ff in range(4):
            f = f0 * 4 + ff
            w = tabf_sm[2 * CAP, f]
            sums = tile(t_hi[0, w], t_lo[0, w], f_hi[f], f_lo[f], kf_row, kf_col, f)
            acc = acc + jnp.where(sub8 == f, sums, 0.0)
        return acc

    for h in range(1, hops + 1):
        final = h == hops
        ways = ((-h, z_plus, up), (h, z_minus, down))
        w_plus[h].wait_recv()
        if not final:
            w_plus[h + 1] = send(two(-h, 0), two(-h - 1, 0), up)
        w_core[-h] = send(two(-h, 0), two(-h, 1), partner)
        if not final:
            w_minus[h].wait_recv()
            if h + 1 < hops:
                w_minus[h + 1] = send(two(h, 0), two(h + 1, 0), down)
            w_core[h] = send(two(h, 0), two(h, 1), partner)
        for p in range(3):
            bx, first = pieces[p]
            rows = pl.ds(first, half)
            for k, (dz, got, onward) in enumerate(ways):
                got[h, p].wait_recv()
                if h + 1 < hops:
                    got[h + 1, p] = send(piece(dz, p), piece(-h - 1 if k == 0 else h + 1, p), onward)
                elif h + 1 == hops:
                    got[hops, p] = send(piece(dz, p, k * quarter, quarter), piece(hops, p, k * quarter, quarter), onward)
            for dz in (-h, h)[: 1 if final else 2]:
                key = hops if final else dz
                if p == 0:
                    post[key] = send(s_raw.at[rel(dz, 0, 0), hi], s_raw.at[rel(dz, 0, 1), hi], mate)
                cores.setdefault(key, []).append(
                    send(s_raw.at[rel(dz, 0, bx), rows], s_raw.at[rel(dz, 1, bx), rows], partner))
            if p == 1:
                for dz in ((0,) if h == 1 else (1 - h, h - 1)):
                    for copy in cores[dz]:
                        copy.wait_recv()
                    norm_lines(dz)
                if h == 2:
                    f_far.wait_recv()

                    def far_unit(i, _):
                        for w in range(sb):
                            f_hi[w], f_lo[w] = unit(f_raw[w], True)
                        return 0

                    lax.fori_loop(0, 1, far_unit, 0)
                if final:
                    for copy in w_core.values():
                        copy.wait_recv()
                    lane8 = lax.broadcasted_iota(I32, (8, N), 1)
                    compact = jnp.zeros((8, N), I32)
                    for r in range(nr):
                        moved = pltpu.roll(tabs[r], lax.rem(r * 4 + N - z * line - (x // 2) * 4, N), 1)
                        compact = jnp.where(lane8 // 4 == r, moved, compact)
                    tabc[...] = compact
                    w_far.wait_recv()
                    far_table = pltpu.make_async_copy(tabf, tabf_sm, loc.at[3])
                    far_table.start()
                    t_pair.wait_recv()
                    norm_t(1)
                    tables = pltpu.make_async_copy(tabc, tabs_sm, loc.at[2])
                    tables.start()
                    far_table.wait()
                    tables.wait()
                    rf0[...] = lax.fori_loop(0, sb // 4, far_tiles, jnp.zeros((8, N), F32))

                    def builds(i, _):
                        j = (hops * 2 - 1 - i) // 2
                        build(jnp.where(i % 2 == 0, j, lax.rem(nz - j, nz)))
                        return 0

                    lax.fori_loop(0, nz - 1, builds, 0)
        for dz in (-h, h)[: 1 if final else 2]:
            key = hops if final else dz
            post[key].wait_recv()
            cores[key].append(send(s_raw.at[rel(dz, 0, 1), hi], s_raw.at[rel(dz, 1, 1), hi], partner))
    for copy in cores[hops]:
        copy.wait_recv()
    norm_lines(hops)

    def last_build(i, _):
        build(hops + i)
        return 0

    lax.fori_loop(0, 1, last_build, 0)

    others = [(dz,) + o for dz in range(nz) for o in four if (dz,) + o != (0, 0, 0)]
    others.sort(key=lambda o: -min(o[0], nz - o[0]))

    def exchange(src, dst, k, to_dev):
        return pltpu.make_async_remote_copy(
            src_ref=src, dst_ref=dst, send_sem=ex_snd.at[k], recv_sem=ex_rcv.at[k],
            device_id=to_dev, device_id_type=MESH)

    def group(j):
        return lax.rem(nz - j, nz), j + 1

    def spread(v, r):
        h, l = halves(v)
        return jnp.where(sub16 == r, h, jnp.where(sub16 == r + 8, l, 0.0)).astype(BF16)

    def product(lhs, tiles):
        o = nn(jnp.concatenate([v for v in lhs for _ in range(2)], axis=1), tiles)
        return o[:8] + o[8:]

    def rows_pass(rp, rpi, rf):
        def body(r0, _):
            j = hops - 1 - r0
            for dz in group(j):
                for flip, bx in four:
                    r = dz * 4 + flip * 2 + bx
                    lhs = []
                    for t in range(PAIR):
                        for u in range(CAP):
                            b, q = tabs_sm[u, lane_of(r, t)], tabs_sm[CAP + u, lane_of(r, t)]
                            lhs.append(spread(ts[t, pl.ds(jnp.maximum(q, 0), 1), :], b))
                    rp[r] = product(lhs, k_row[dz * 2 + flip, pl.ds(bx * near * 2 * N, near * 2 * N), :])
            for dz in group(j):
                send_rows(rp, rpi, dz)
            return 0

        lax.fori_loop(0, hops, body, 0)
        lhs = [spread(ts[0, pl.ds(tabf_sm[2 * CAP, f], 1), :], f) for f in range(sb)]
        rf[...] = product(lhs, kf_row[...])

    def cols_pass(so, ss, sf, far_copy):
        def body(j, accs):
            accs = list(accs)
            for dz in group(j):
                for flip, bx in four:
                    copy = from_line(so, ss, ag_snd, ag_rcv, dz, flip, bx, True)
                    if (flip, bx) == (0, 0):
                        pl.when(dz > 0)(copy.wait_recv)
                    else:
                        copy.wait_recv()
            for dz in group(j):
                for i in range(4):
                    ssl[dz * 4 + i] = ss[dz * 4 + i]
            for dz in group(j):
                for flip in range(2):
                    lhs = []
                    slots = [(bx, t, u) for bx in range(2) for t in range(PAIR) for u in range(CAP)]
                    for k, (bx, t, u) in enumerate(slots):
                        r = dz * 4 + flip * 2 + bx
                        b = tabs_sm[u, lane_of(r, t)]
                        lhs.append(spread(ssl[r, pl.ds(jnp.maximum(b, 0), 1), :], k))
                    o = product(lhs, k_col[dz * 2 + flip])
                    for k, (bx, t, u) in enumerate(slots):
                        q = tabs_sm[CAP + u, lane_of(dz * 4 + flip * 2 + bx, t)]
                        accs[t] = accs[t] + jnp.where(sub32 == q, o[k : k + 1], 0.0)
            return tuple(accs)

        zero = jnp.zeros((tb_dev, N), F32)
        accs = list(lax.fori_loop(0, hops, body, (zero,) * PAIR))
        far_copy.wait_recv()
        lhs = [spread(sf[f : f + 1, :], f) for f in range(sb)]
        o = product(lhs, kf_col[...])
        for f in range(sb):
            accs[0] = accs[0] + jnp.where(sub32 == tabf_sm[2 * CAP, f], o[f : f + 1], 0.0)
        return accs

    mass_pair.wait_recv()
    for it, (rp, rpi, rf, rfi, so, ss, sf, co, ci) in enumerate((
        (rp0, rpi0, rf0, rfi0, so0, ss0, sf0, co0, ci0),
        (rp1, rpi1, rf1, rfi1, so1, ss1, sf1, co1, ci1),
    )):
        last = it == ITERS - 1
        far_rows = exchange(rf, rfi, 0, behind)
        far_scale = exchange(so, sf, 1, ahead)
        if it > 0:
            rows_pass(rp, rpi, rf)
        far_rows.start()
        total = rp[0]
        for o in others[::-1]:
            from_line(rp, rpi, rs_snd, rs_rcv, *o).wait_recv()
        far_rows.wait_recv()
        total = total + rfi[...]
        for o in others:
            total = total + rpi[rel(*o)]
        scale = smass[...] / (DUSTBIN + total)
        so[...] = scale
        ss[0] = scale
        if last:
            out[:sb] = scale
        for o in others:
            to_line(so, ss, ag_snd, ag_rcv, *o, True).start()
        far_scale.start()
        accs = cols_pass(so, ss, sf, far_scale)
        co[1] = accs[1]
        if last:
            swap = exchange(co.at[1], ci.at[1], 3, pair)
        else:
            co[0] = accs[0]
            swap = exchange(co, ci, 2, pair)
        swap.start()
        for o in others:
            to_line(rp, rpi, rs_snd, rs_rcv, *o).wait_send()
            to_line(so, ss, ag_snd, ag_rcv, *o, True).wait_send()
        far_rows.wait_send()
        far_scale.wait_send()
        swap.wait_recv()
        scale = tmass[...] / (DUSTBIN + (accs[0] + ci[1]))
        if last:
            out[sb:] = scale
        else:
            ts[0] = scale
            ts[1] = tmass_pair[...] / (DUSTBIN + (accs[1] + ci[0]))
        swap.wait_send()
    for copy in sent:
        copy.wait_send()
    assert count[0] == COPIES


def local(ng, nz, semb, temb, smass, tmass, cdev, cblk):
    sb, tb = semb.shape[0], temb.shape[0]
    nr = 4 * nz
    slots = 2 * PAIR * CAP * 2 * N
    vm = pltpu.VMEM
    dma = pltpu.SemaphoreType.DMA
    tile = (N, N)
    blocks = vm((nr, sb, N), F32)
    source, target = vm((sb, N), F32), vm((tb, N), F32)
    pair = vm((PAIR, tb, N), F32)
    scratch = [
        vm((nr, sb) + tile, F32), vm((PAIR, tb) + tile, F32), vm((sb,) + tile, F32),
        vm((nr * sb,) + tile, BF16), vm((nr * sb,) + tile, BF16),
        vm((PAIR, tb) + tile, BF16), vm((PAIR, tb) + tile, BF16),
        vm((sb,) + tile, BF16), vm((sb,) + tile, BF16),
        vm((nr // 2, slots, N), BF16), vm((nr // 2, slots, N), BF16),
        vm((sb * 2 * N, N), BF16), vm((sb * 2 * N, N), BF16),
        vm((8, N), I32), vm((nr, 8, N), I32), vm((8, N), I32), vm((8, N), I32),
        pltpu.SMEM((8, N), I32), pltpu.SMEM((8, N), I32),
    ]
    scratch += [blocks] * 7 + [source] * 8 + [pair] * 5
    scratch += [vm(a.shape, a.dtype) for a in (smass, tmass, cdev, cblk)] + [target]
    scratch += [dma((COPIES,))] * 2 + [dma((nr,))] * 4 + [dma((4,))] * 2 + [dma((8,))]
    any_, vmem = pl.BlockSpec(memory_space=pl.ANY), pl.BlockSpec(memory_space=pltpu.VMEM)
    both = pl.pallas_call(
        functools.partial(kernel, ng, nz, sb, tb),
        out_shape=jax.ShapeDtypeStruct((sb + tb, N), F32),
        in_specs=[any_] * 6,
        out_specs=vmem,
        scratch_shapes=scratch,
        compiler_params=pltpu.CompilerParams(
            collective_id=0, has_side_effects=True, vmem_limit_bytes=VMEM_BYTES),
        name="sinkhorn",
    )(semb, temb, smass, tmass, cdev, cblk)

    def split(both_ref, src_ref, tgt_ref):
        src_ref[...] = both_ref[:sb]
        tgt_ref[...] = both_ref[sb:]

    return pl.pallas_call(
        split,
        out_shape=(jax.ShapeDtypeStruct(smass.shape, F32), jax.ShapeDtypeStruct(tmass.shape, F32)),
        in_specs=[vmem],
        out_specs=(vmem, vmem),
        name="split",
    )(both)


def solution(mesh):
    placed = (
        P(("group", "dev"), None, None),
        P(("group", "dev"), None, None),
        P(("group", "dev"), None),
        P(("group", "dev"), None),
        P(("group", "dev"), None),
        P(("group", "dev"), None),
    )
    ng, nz = mesh.shape["group"], mesh.shape["dev"] // (2 * NX)
    return jax.shard_map(
        functools.partial(local, ng, nz),
        mesh=mesh,
        in_specs=placed,
        out_specs=(P(("group", "dev"), None), P(("group", "dev"), None)),
        check_vma=False,
    )
```

time: 114 us -> 118 us (1.035)
  Pallas kernels: 114 us -> 117 us
    pallas_call x1, Pallas kernels: 112 us -> 116 us  [local(): pl.pallas_call(functools.partial(kernel, ng, nz, sb, tb), out_shape=jax.S...]
where the time goes in v4:
time: 118 us
  Pallas kernels  117 us (99%)
    pallas_call x1, Pallas kernels, local(): pl.pallas_call(functools.partial(kernel, ng, nz, sb, tb), out_shape=jax.S...  116 us

profile of v4, /device:TPU:1, one launch (start us, length us, event | category | flops | bytes accessed | tf_op | source)
XLA Modules:
  0.0 117.8 jit_solution(10170360571768256696)
XLA Ops:
  0.6 115.8 %sinkhorn.1.both_ref = f32[40,128]{1,0:T(8,128)} custom-call(f32[8,128,128]{2,1,0:T(8,128)} %refs_0_.1, f32[32,128,128]{2,1,0:T(8,128)} %refs_1_.1, f32[8,128]{1,0:T(8,128)} %refs_2_.1, f32[32,128]{1,0:T(8,128)} %refs_3_.1, s32[8,7]{1,0:T(8,128)} %refs_4_.1, s32[8,8]{1,0:T(8,128)} %refs_5_.1), custom_call_target="tpu_custom_call" | custom-call | tf_op jit(solution)/shard_map/sinkhorn/pallas_call | solution.py:478
  116.4 1.3 %split.1 = (f32[8,128]{1,0:T(8,128)}, f32[32,128]{1,0:T(8,128)}) custom-call(f32[40,128]{1,0:T(8,128)} %sinkhorn.1.both_ref), custom_call_target="tpu_custom_call" | custom-call | tf_op jit(solution)/shard_map/split/pallas_call | solution.py:493

commit v5 on v4

--- a/solution.py
+++ b/solution.py
@@ -147,14 +147,14 @@
         h = v.astype(BF16)
         return h, (v - h.astype(F32)).astype(BF16)
 
-    def norm_lines(dz):
-        def one(i, _):
-            r = rel(dz, 0, 0) + i
+    def norm_lines(dz, bx):
+        def one(flip, _):
+            r = rel(dz, 0, bx) + flip * 2
             for w in range(sb):
                 s_hi[r * sb + w], s_lo[r * sb + w] = unit(s_raw[r, w], True)
             return 0
 
-        lax.fori_loop(0, 4, one, 0)
+        lax.fori_loop(0, 2, one, 0)
 
     def norm_t(t):
         def one(i, _):
@@ -201,39 +201,74 @@
         r = dz * 4 + flip * 2 + bx
         back = lax.rem(nz - dz, nz) * 4 + flip * 2 + bx
         return pltpu.make_async_remote_copy(
-            src_ref=src if whole else src.at[r], dst_ref=dst.at[back], send_sem=snds.at[r],
+            src_ref=src if whole else src.at[r], dst_ref=dst.at[back], send_sem=snds.at[0],
             recv_sem=rcvs.at[back], device_id=dev(dz, flip, bx), device_id_type=MESH)
 
     def from_line(src, dst, snds, rcvs, dz, flip, bx, whole=False):
         r = dz * 4 + flip * 2 + bx
         return pltpu.make_async_remote_copy(
-            src_ref=src if whole else src.at[r], dst_ref=dst.at[r], send_sem=snds.at[r],
+            src_ref=src if whole else src.at[r], dst_ref=dst.at[r], send_sem=snds.at[0],
             recv_sem=rcvs.at[r], device_id=dev(dz, flip, bx), device_id_type=MESH)
 
     four = tuple((flip, bx) for flip in range(2) for bx in range(2))
 
-    def send_rows(rp, rpi, dz):
+    def send_rows(rp, rpi, dz, bxs=(0, 1)):
         for flip, bx in four:
-            copy = to_line(rp, rpi, rs_snd, rs_rcv, dz, flip, bx)
-            if (flip, bx) == (0, 0):
-                pl.when(dz > 0)(copy.start)
-            else:
-                copy.start()
-
-    def build(dz):
+            if bx in bxs:
+                copy = to_line(rp, rpi, rs_snd, rs_rcv, dz, flip, bx)
+                if (flip, bx) == (0, 0):
+                    pl.when(dz > 0)(copy.start)
+                else:
+                    copy.start()
+
+    def build(dz, dist, bxs, targets, first, done):
         for flip in range(2):
-            for bx in range(2):
+            for bx in bxs:
                 r = dz * 4 + flip * 2 + bx
                 acc = jnp.zeros((8, N), F32)
-                for t in range(PAIR):
+                for t in targets:
                     for u in range(CAP):
-                        b, q = tabs_sm[u, lane_of(r, t)], tabs_sm[CAP + u, lane_of(r, t)]
+                        b, q = tabs_sm[dist, u, lane_of(r, t)], tabs_sm[dist, CAP + u, lane_of(r, t)]
                         s, w = r * sb + jnp.maximum(b, 0), jnp.maximum(q, 0)
                         sums = tile(t_hi[t, w], t_lo[t, w], s_hi[s], s_lo[s], k_row.at[dz * 2 + flip],
                                     k_col.at[dz * 2 + flip], bx * near + t * CAP + u)
                         acc = acc + jnp.where(sub8 == b, sums, 0.0)
-                rp0[r] = acc
-        send_rows(rp0, rpi0, dz)
+                rp0[r] = acc if first else rp0[r] + acc
+        if done:
+            send_rows(rp0, rpi0, dz, bxs)
+
+    def builds(first_place, places, targets, first, done):
+        def one(i, _):
+            p = first_place + i
+            dist = (p + 1) // 2
+            dz = jnp.where(p % 2 == 1, dist, lax.rem(nz - dist, nz))
+            build(dz, dist, (0, 1), targets, first, done)
+            return 0
+
+        lax.fori_loop(0, places, one, 0)
+
+    def last_build(bx):
+        def one(i, _):
+            build(hops + i, hops, (bx,), (0, 1), True, True)
+            return 0
+
+        lax.fori_loop(0, 1, one, 0)
+
+    lane8 = lax.broadcasted_iota(I32, (8, N), 1)
+
+    def compact(dist):
+        places = (0,) if dist == 0 else (hops,) if dist == hops else (-dist, dist)
+        part = jnp.zeros((8, N), I32)
+        for dz in places:
+            w_core[dz].wait_recv()
+            for i in range(4):
+                r = rel(dz, 0, 0) + i
+                moved = pltpu.roll(tabs[r], lax.rem(r * 4 + N - z * line - (x // 2) * 4, N), 1)
+                part = jnp.where(lane8 // 4 == r, moved, part)
+        tabc[dist] = part
+
+    def table_copy(dist):
+        return pltpu.make_async_copy(tabc.at[dist], tabs_sm.at[dist], loc.at[2])
 
     def far_tiles(f0, acc):
         for ff in range(4):
@@ -249,7 +284,7 @@
         w_plus[h].wait_recv()
         if not final:
             w_plus[h + 1] = send(two(-h, 0), two(-h - 1, 0), up)
-        w_core[-h] = send(two(-h, 0), two(-h, 1), partner)
+        w_core[hops if final else -h] = send(two(-h, 0), two(-h, 1), partner)
         if not final:
             w_minus[h].wait_recv()
             if h + 1 < hops:
@@ -270,12 +305,24 @@
                     post[key] = send(s_raw.at[rel(dz, 0, 0), hi], s_raw.at[rel(dz, 0, 1), hi], mate)
                 cores.setdefault(key, []).append(
                     send(s_raw.at[rel(dz, 0, bx), rows], s_raw.at[rel(dz, 1, bx), rows], partner))
-            if p == 1:
-                for dz in ((0,) if h == 1 else (1 - h, h - 1)):
+            if p == (0 if final else 1):
+                dist = h - 1
+                compact(dist)
+                for dz in ((0,) if dist == 0 else (-dist, dist)):
                     for copy in cores[dz]:
                         copy.wait_recv()
-                    norm_lines(dz)
+                    norm_lines(dz, 0)
+                    if dz == (0 if dist == 0 else -dist):
+                        table_copy(dist).start()
+                    norm_lines(dz, 1)
+                table_copy(dist).wait()
+                place, places = (0, 1) if dist == 0 else (2 * dist - 1, 2)
+                if h < hops - 1:
+                    builds(place, places, (0,), True, False)
                 if h == 2:
+                    w_far.wait_recv()
+                    far_table = pltpu.make_async_copy(tabf, tabf_sm, loc.at[3])
+                    far_table.start()
                     f_far.wait_recv()
 
                     def far_unit(i, _):
@@ -284,45 +331,30 @@
                         return 0
 
                     lax.fori_loop(0, 1, far_unit, 0)
-                if final:
-                    for copy in w_core.values():
-                        copy.wait_recv()
-                    lane8 = lax.broadcasted_iota(I32, (8, N), 1)
-                    compact = jnp.zeros((8, N), I32)
-                    for r in range(nr):
-                        moved = pltpu.roll(tabs[r], lax.rem(r * 4 + N - z * line - (x // 2) * 4, N), 1)
-                        compact = jnp.where(lane8 // 4 == r, moved, compact)
-                    tabc[...] = compact
-                    w_far.wait_recv()
-                    far_table = pltpu.make_async_copy(tabf, tabf_sm, loc.at[3])
-                    far_table.start()
+                    far_table.wait()
+                    rf0[...] = lax.fori_loop(0, sb // 4, far_tiles, jnp.zeros((8, N), F32))
+                if h == hops - 1:
+                    builds(place, places, (0,), True, False)
                     t_pair.wait_recv()
                     norm_t(1)
-                    tables = pltpu.make_async_copy(tabc, tabs_sm, loc.at[2])
-                    tables.start()
-                    far_table.wait()
-                    tables.wait()
-                    rf0[...] = lax.fori_loop(0, sb // 4, far_tiles, jnp.zeros((8, N), F32))
-
-                    def builds(i, _):
-                        j = (hops * 2 - 1 - i) // 2
-                        build(jnp.where(i % 2 == 0, j, lax.rem(nz - j, nz)))
-                        return 0
-
-                    lax.fori_loop(0, nz - 1, builds, 0)
+                    builds(0, place + places, (1,), False, True)
+                if final:
+                    builds(place, places, (0, 1), True, True)
+        if final:
+            compact(hops)
+            for copy in cores[hops]:
+                copy.wait_recv()
+            norm_lines(hops, 0)
+            table_copy(hops).start()
+            table_copy(hops).wait()
+            last_build(0)
         for dz in (-h, h)[: 1 if final else 2]:
             key = hops if final else dz
             post[key].wait_recv()
             cores[key].append(send(s_raw.at[rel(dz, 0, 1), hi], s_raw.at[rel(dz, 1, 1), hi], partner))
-    for copy in cores[hops]:
-        copy.wait_recv()
-    norm_lines(hops)
-
-    def last_build(i, _):
-        build(hops + i)
-        return 0
-
-    lax.fori_loop(0, 1, last_build, 0)
+    cores[hops][-1].wait_recv()
+    norm_lines(hops, 1)
+    last_build(1)
 
     others = [(dz,) + o for dz in range(nz) for o in four if (dz,) + o != (0, 0, 0)]
     others.sort(key=lambda o: -min(o[0], nz - o[0]))
@@ -333,7 +365,7 @@
             device_id=to_dev, device_id_type=MESH)
 
     def group(j):
-        return lax.rem(nz - j, nz), j + 1
+        return (lax.rem(nz - j, nz), j), (j + 1, j + 1)
 
     def spread(v, r):
         h, l = halves(v)
@@ -346,16 +378,16 @@
     def rows_pass(rp, rpi, rf):
         def body(r0, _):
             j = hops - 1 - r0
-            for dz in group(j):
+            for dz, dist in group(j):
                 for flip, bx in four:
                     r = dz * 4 + flip * 2 + bx
                     lhs = []
                     for t in range(PAIR):
                         for u in range(CAP):
-                            b, q = tabs_sm[u, lane_of(r, t)], tabs_sm[CAP + u, lane_of(r, t)]
+                            b, q = tabs_sm[dist, u, lane_of(r, t)], tabs_sm[dist, CAP + u, lane_of(r, t)]
                             lhs.append(spread(ts[t, pl.ds(jnp.maximum(q, 0), 1), :], b))
                     rp[r] = product(lhs, k_row[dz * 2 + flip, pl.ds(bx * near * 2 * N, near * 2 * N), :])
-            for dz in group(j):
+            for dz, _ in group(j):
                 send_rows(rp, rpi, dz)
             return 0
 
@@ -366,27 +398,27 @@
     def cols_pass(so, ss, sf, far_copy):
         def body(j, accs):
             accs = list(accs)
-            for dz in group(j):
+            for dz, _ in group(j):
                 for flip, bx in four:
                     copy = from_line(so, ss, ag_snd, ag_rcv, dz, flip, bx, True)
                     if (flip, bx) == (0, 0):
                         pl.when(dz > 0)(copy.wait_recv)
                     else:
                         copy.wait_recv()
-            for dz in group(j):
+            for dz, _ in group(j):
                 for i in range(4):
                     ssl[dz * 4 + i] = ss[dz * 4 + i]
-            for dz in group(j):
+            for dz, dist in group(j):
                 for flip in range(2):
                     lhs = []
                     slots = [(bx, t, u) for bx in range(2) for t in range(PAIR) for u in range(CAP)]
                     for k, (bx, t, u) in enumerate(slots):
                         r = dz * 4 + flip * 2 + bx
-                        b = tabs_sm[u, lane_of(r, t)]
+                        b = tabs_sm[dist, u, lane_of(r, t)]
                         lhs.append(spread(ssl[r, pl.ds(jnp.maximum(b, 0), 1), :], k))
                     o = product(lhs, k_col[dz * 2 + flip])
                     for k, (bx, t, u) in enumerate(slots):
-                        q = tabs_sm[CAP + u, lane_of(dz * 4 + flip * 2 + bx, t)]
+                        q = tabs_sm[dist, CAP + u, lane_of(dz * 4 + flip * 2 + bx, t)]
                         accs[t] = accs[t] + jnp.where(sub32 == q, o[k : k + 1], 0.0)
             return tuple(accs)
 
@@ -433,9 +465,8 @@
             co[0] = accs[0]
             swap = exchange(co, ci, 2, pair)
         swap.start()
-        for o in others:
-            to_line(rp, rpi, rs_snd, rs_rcv, *o).wait_send()
-            to_line(so, ss, ag_snd, ag_rcv, *o, True).wait_send()
+        for left, sem in ((rp, rs_snd), (ss, ag_snd)):
+            pltpu.make_async_copy(left.at[pl.ds(1, nr - 1)], left.at[pl.ds(1, nr - 1)], sem.at[0]).wait()
         far_rows.wait_send()
         far_scale.wait_send()
         swap.wait_recv()
@@ -468,12 +499,12 @@
         vm((sb,) + tile, BF16), vm((sb,) + tile, BF16),
         vm((nr // 2, slots, N), BF16), vm((nr // 2, slots, N), BF16),
         vm((sb * 2 * N, N), BF16), vm((sb * 2 * N, N), BF16),
-        vm((8, N), I32), vm((nr, 8, N), I32), vm((8, N), I32), vm((8, N), I32),
-        pltpu.SMEM((8, N), I32), pltpu.SMEM((8, N), I32),
+        vm((8, N), I32), vm((nr, 8, N), I32), vm((8, N), I32), vm((nz // 2 + 1, 8, N), I32),
+        pltpu.SMEM((nz // 2 + 1, 8, N), I32), pltpu.SMEM((8, N), I32),
     ]
     scratch += [blocks] * 7 + [source] * 8 + [pair] * 5
     scratch += [vm(a.shape, a.dtype) for a in (smass, tmass, cdev, cblk)] + [target]
-    scratch += [dma((COPIES,))] * 2 + [dma((nr,))] * 4 + [dma((4,))] * 2 + [dma((8,))]
+    scratch += [dma((COPIES,))] * 2 + [dma((1,)), dma((nr,)), dma((1,)), dma((nr,))] + [dma((4,))] * 2 + [dma((8,))]
     any_, vmem = pl.BlockSpec(memory_space=pl.ANY), pl.BlockSpec(memory_space=pltpu.VMEM)
     both = pl.pallas_call(
         functools.partial(kernel, ng, nz, sb, tb),

time: 118 us -> 113 us (0.958)
  Pallas kernels: 117 us -> 113 us
    pallas_call x1, Pallas kernels: 116 us -> 111 us  [local(): pl.pallas_call(functools.partial(kernel, ng, nz, sb, tb), out_shape=jax.S...]
where the time goes in v5:
time: 113 us
  Pallas kernels  113 us (100%)
    pallas_call x1, Pallas kernels, local(): pl.pallas_call(functools.partial(kernel, ng, nz, sb, tb), out_shape=jax.S...  111 us

profile of v5, /device:TPU:1, one launch (start us, length us, event | category | flops | bytes accessed | tf_op | source)
XLA Modules:
  0.0 113.1 jit_solution(11185201655920256232)
XLA Ops:
  0.6 111.2 %sinkhorn.1.both_ref = f32[40,128]{1,0:T(8,128)} custom-call(f32[8,128,128]{2,1,0:T(8,128)} %refs_0_.1, f32[32,128,128]{2,1,0:T(8,128)} %refs_1_.1, f32[8,128]{1,0:T(8,128)} %refs_2_.1, f32[32,128]{1,0:T(8,128)} %refs_3_.1, s32[8,7]{1,0:T(8,128)} %refs_4_.1, s32[8,8]{1,0:T(8,128)} %refs_5_.1), custom_call_target="tpu_custom_call" | custom-call | tf_op jit(solution)/shard_map/sinkhorn/pallas_call | solution.py:509
  111.8 1.3 %split.1 = (f32[8,128]{1,0:T(8,128)}, f32[32,128]{1,0:T(8,128)}) custom-call(f32[40,128]{1,0:T(8,128)} %sinkhorn.1.both_ref), custom_call_target="tpu_custom_call" | custom-call | tf_op jit(solution)/shard_map/split/pallas_call | solution.py:524

commit v6 on v5

v6 whole, which is shorter than its diff:
```python
import functools

import jax
import jax.numpy as jnp
from jax import lax
from jax.experimental import pallas as pl
from jax.experimental.pallas import tpu as pltpu
from jax.sharding import PartitionSpec as P

MESH = pl.DeviceIdType.MESH
N = 128
NX = 4
NEAR = 7
CAP = 2
TARGETS = 4
VMEM_BYTES = 62 * 1024 * 1024
ITERS = 2
EMPTY = -64
COPIES = 49
DUSTBIN = 0.5
EPSILON = 1e-6
GAIN = 1.0 / (N * 0.1)
SHARE = 1.0 / (8.0 * N)

F32, BF16, I32 = jnp.float32, jnp.bfloat16, jnp.int32


def nn(a, b):
    return lax.dot_general(a, b, (((1,), (0,)), ((), ())), preferred_element_type=F32)


def halves(v):
    hi = v.astype(BF16).astype(F32)
    return hi, v - hi


def kernel(ng, nz, sb, tb_dev, *refs):
    (semb, temb, smass_in, tmass_in, cdev_in, cblk_in, out,
     s_raw, t_raw, f_raw, s_hi, s_lo, t_hi, t_lo, f_hi, f_lo, k_row, k_col, kf_row, kf_col,
     tab, tabs, tabf, tabc, tabs_sm, tabf_sm,
     rp0, rp1, rpi0, rpi1, ss0, ss1, ssl, rf0, rf1, rfi0, rfi1, so0, so1, sf0, sf1,
     co0, co1, ci0, ci1, wo0, wo1, wi0, wi1, ts, smass, cdev, cblk, tmass,
     snd, rcv, rs_snd, rs_rcv, ag_snd, ag_rcv, ex_snd, ex_rcv, loc) = refs
    nr = 2 * nz
    hops = nz // 2
    half = sb // 2
    quarter = sb // 4
    line = 2 * NX
    g, d = lax.axis_index("group"), lax.axis_index("dev")
    z, x, c = d // line, (d // 2) % NX, d % 2

    def at(zz, xx, cc):
        return (g, zz * line + xx * 2 + cc)

    def dev(dz, bx):
        return at(lax.rem(z + dz, nz), NX - 1 - x if bx else x, c)

    def rel(dz, bx):
        return (dz % nz) * 2 + bx

    up, down, mate = dev(1, 0), dev(nz - 1, 0), dev(0, 1)
    partner = at(z, x, 1 - c)
    pair = at(z, x + 1 - 2 * lax.rem(x, 2), c)
    ahead, behind = (lax.rem(g + 1, ng), d), (lax.rem(g + ng - 1, ng), d)

    count = [0]
    sent = []

    def send(src, dst, to_dev):
        k = count[0]
        count[0] += 1
        copy = pltpu.make_async_remote_copy(
            src_ref=src, dst_ref=dst, send_sem=snd.at[k], recv_sem=rcv.at[k],
            device_id=to_dev, device_id_type=MESH)
        copy.start()
        sent.append(copy)
        return copy

    barrier = pltpu.get_barrier_semaphore()
    greeted = (up, down, mate, pair, partner, ahead, behind)
    for other in greeted:
        pl.semaphore_signal(barrier, inc=1, device_id=other, device_id_type=MESH)
    own_s = pltpu.make_async_copy(semb, s_raw.at[0], loc.at[0])
    own_t = pltpu.make_async_copy(temb, t_raw.at[0], loc.at[1])
    small = [pltpu.make_async_copy(a, b, loc.at[4 + i]) for i, (a, b) in enumerate(
        ((cdev_in, cdev), (cblk_in, cblk), (smass_in, smass), (tmass_in, tmass.at[0])))]
    for copy in small:
        copy.start()
    own_s.start()
    own_t.start()
    for copy in small:
        copy.wait()

    lane = lax.broadcasted_iota(I32, (1, N), 1)
    run = jnp.zeros((1, N), I32)
    rows = [jnp.full((1, N), EMPTY, I32) for _ in range(2 * CAP)]
    far = jnp.zeros((1, N), I32)
    for b in range(sb):
        hit = jnp.zeros((1, N), I32)
        which = jnp.zeros((1, N), I32)
        for k in range(NEAR):
            m = cdev[b : b + 1, k : k + 1] == lane
            hit = jnp.where(m, 1, hit)
            which = jnp.where(m, cblk[b : b + 1, k : k + 1], which)
        for u in range(CAP):
            m = (hit == 1) & (run == u)
            rows[u] = jnp.where(m, b, rows[u])
            rows[CAP + u] = jnp.where(m, which, rows[CAP + u])
        run = run + hit
        far = jnp.where(lane == b, cblk[b : b + 1, NEAR : NEAR + 1], far)
    table = jnp.concatenate(rows + [far] + [jnp.zeros((1, N), I32)] * (7 - 2 * CAP), axis=0)
    tab[...] = table
    tabs[0] = table

    pl.semaphore_wait(barrier, len(greeted))

    lo, hi = pl.ds(0, half), pl.ds(half, half)
    pieces = ((0, half), (0, 0), (1, 0))
    z_plus, z_minus = {}, {}

    def piece(dz, p, start=0, size=half):
        bx, first = pieces[p]
        return s_raw.at[rel(dz, bx), pl.ds(first + start, size)]

    w_mate = send(tab, tabs.at[1], mate)
    pre = send(semb.at[lo], s_raw.at[rel(0, 1), lo], mate)
    for p in (0, 1):
        part = semb.at[pl.ds(pieces[p][1], half)]
        z_plus[1, p] = send(part, piece(-1, p), up)
        z_minus[1, p] = send(part, piece(1, p), down)
    post = {0: send(semb.at[hi], s_raw.at[rel(0, 1), hi], mate)}
    t_pair = send(temb, t_raw.at[1], pair)
    mass_pair = send(tmass_in, tmass.at[1], pair)
    t_core = send(temb, t_raw.at[2], partner)
    mass_core = send(tmass_in, tmass.at[2], partner)
    w_far = send(tab, tabf, ahead)
    f_far = send(semb, f_raw, ahead)
    w_plus, w_minus = {}, {}

    def two(dz):
        return tabs.at[pl.ds(rel(dz, 0), 2)]

    def place(p):
        dist = (p + 1) // 2
        return jnp.where(p % 2 == 1, dist, lax.rem(nz - dist, nz)), dist

    def unit(v, turned):
        if turned:
            v = v.T
        v = v * lax.rsqrt(jnp.mean(v * v, axis=0 if turned else 1, keepdims=True) + EPSILON)
        h = v.astype(BF16)
        return h, (v - h.astype(F32)).astype(BF16)

    def norm_lines(first_line, lines):
        def one(i, _):
            dz, _dist = place((first_line + i) // 2)
            r = dz * 2 + (first_line + i) % 2
            for w in range(sb):
                s_hi[r * sb + w], s_lo[r * sb + w] = unit(s_raw[r, w], True)
            return 0

        lax.fori_loop(0, lines, one, 0)

    def norm_t(t):
        def one(i, _):
            for w in range(8):
                t_hi[t, i * 8 + w], t_lo[t, i * 8 + w] = unit(t_raw[t, i * 8 + w], False)
            return 0

        lax.fori_loop(0, tb_dev // 8, one, 0)

    w_mate.wait_recv()
    w_plus[1] = send(two(0), two(-1), up)
    w_minus[1] = send(two(0), two(1), down)
    pre.wait_recv()
    z_plus[1, 2] = send(piece(0, 2), piece(-1, 2), up)
    z_minus[1, 2] = send(piece(0, 2), piece(1, 2), down)
    own_t.wait()
    norm_t(0)
    t_core.wait_recv()
    norm_t(2)
    own_s.wait()
    post[0].wait_recv()

    sub8 = lax.broadcasted_iota(I32, (8, N), 0)
    sub16 = lax.broadcasted_iota(I32, (16, N), 0)
    sub32 = lax.broadcasted_iota(I32, (tb_dev, N), 0)

    def lane_of(r, t):
        return r * 4 + lax.rem(x + t, 2) * 2 + (c if t < 2 else 1 - c)

    def two_terms(v, ref, k):
        h = v.astype(BF16)
        ref[pl.ds(k * 2 * N, N), :] = h
        ref[pl.ds(k * 2 * N + N, N), :] = (v - h.astype(F32)).astype(BF16)

    def tile(b_hi, b_lo, a_hi, a_lo, row, col, k):
        dots = nn(b_hi, a_hi) + (nn(b_lo, a_hi) + nn(b_hi, a_lo))
        e = jnp.exp(dots * GAIN) * SHARE
        two_terms(e, row, k)
        two_terms(e.T, col, k)
        return jnp.sum(e, axis=0, keepdims=True)

    def to_line(src, dst, snds, rcvs, dz, bx, whole=False):
        r, back = dz * 2 + bx, lax.rem(nz - dz, nz) * 2 + bx
        return pltpu.make_async_remote_copy(
            src_ref=src if whole else src.at[r], dst_ref=dst.at[back], send_sem=snds.at[0],
            recv_sem=rcvs.at[back], device_id=dev(dz, bx), device_id_type=MESH)

    def from_line(src, dst, snds, rcvs, dz, bx, whole=False):
        r = dz * 2 + bx
        return pltpu.make_async_remote_copy(
            src_ref=src if whole else src.at[r], dst_ref=dst.at[r], send_sem=snds.at[0],
            recv_sem=rcvs.at[r], device_id=dev(dz, bx), device_id_type=MESH)

    def send_rows(rp, rpi, dz, bxs=(0, 1)):
        for bx in bxs:
            copy = to_line(rp, rpi, rs_snd, rs_rcv, dz, bx)
            if bx == 0:
                pl.when(dz > 0)(copy.start)
            else:
                copy.start()

    def build(dz, dist, bxs, targets, first, done):
        for bx in bxs:
            r = dz * 2 + bx
            acc = jnp.zeros((8, N), F32)
            for t in targets:
                for u in range(CAP):
                    b, q = tabs_sm[dist, u, lane_of(r, t)], tabs_sm[dist, CAP + u, lane_of(r, t)]
                    s, w = r * sb + jnp.maximum(b, 0), jnp.maximum(q, 0)
                    sums = tile(t_hi[t, w], t_lo[t, w], s_hi[s], s_lo[s], k_row.at[r], k_col.at[r], t * CAP + u)
                    acc = acc + jnp.where(sub8 == b, sums, 0.0)
            rp0[r] = acc if first else rp0[r] + acc
        if done:
            send_rows(rp0, rpi0, dz, bxs)

    def builds(first_place, places, targets, first, done):
        def one(i, _):
            dz, dist = place(first_place + i)
            build(dz, dist, (0, 1), targets, first, done)
            return 0

        lax.fori_loop(0, places, one, 0)

    def last_build(bx):
        def one(i, _):
            build(hops + i, hops, (bx,), range(TARGETS), True, True)
            return 0

        lax.fori_loop(0, 1, one, 0)

    lane8 = lax.broadcasted_iota(I32, (8, N), 1)

    def compact(dist):
        part = jnp.zeros((8, N), I32)
        for dz in (0,) if dist == 0 else (hops,) if dist == hops else (-dist, dist):
            for bx in range(2):
                r = rel(dz, bx)
                moved = pltpu.roll(tabs[r], lax.rem(r * 4 + N - z * line - (x // 2) * 4, N), 1)
                part = jnp.where(lane8 // 4 == r, moved, part)
        tabc[dist] = part

    def table_copy(dist):
        return pltpu.make_async_copy(tabc.at[dist], tabs_sm.at[dist], loc.at[2])

    def far_tiles(f0, acc):
        for ff in range(4):
            f = f0 * 4 + ff
            w = tabf_sm[2 * CAP, f]
            sums = tile(t_hi[0, w], t_lo[0, w], f_hi[f], f_lo[f], kf_row, kf_col, f)
            acc = acc + jnp.where(sub8 == f, sums, 0.0)
        return acc

    for h in range(1, hops + 1):
        final = h == hops
        w_plus[h].wait_recv()
        if not final:
            w_plus[h + 1] = send(two(-h), two(-h - 1), up)
            w_minus[h].wait_recv()
            if h + 1 < hops:
                w_minus[h + 1] = send(two(h), two(h + 1), down)
        for p in range(3):
            for k, (dz, got, onward) in enumerate(((-h, z_plus, up), (h, z_minus, down))):
                got[h, p].wait_recv()
                if h + 1 < hops:
                    got[h + 1, p] = send(piece(dz, p), piece(-h - 1 if k == 0 else h + 1, p), onward)
                elif h + 1 == hops:
                    got[hops, p] = send(piece(dz, p, k * quarter, quarter), piece(hops, p, k * quarter, quarter), onward)
            if p == 0:
                for dz in (-h, h)[: 1 if final else 2]:
                    post[dz] = send(s_raw.at[rel(dz, 0), hi], s_raw.at[rel(dz, 1), hi], mate)
            if p == (0 if final else 1):
                dist = h - 1
                first, places = (0, 1) if dist == 0 else (2 * dist - 1, 2)
                compact(dist)
                norm_lines(2 * first, places)
                table_copy(dist).start()
                norm_lines(2 * first + places, places)
                table_copy(dist).wait()
                if not final:
                    builds(first, places, (0, 2), True, False)
                if h == 2:
                    w_far.wait_recv()
                    far_table = pltpu.make_async_copy(tabf, tabf_sm, loc.at[3])
                    far_table.start()
                    f_far.wait_recv()

                    def far_unit(i, _):
                        for w in range(sb):
                            f_hi[w], f_lo[w] = unit(f_raw[w], True)
                        return 0

                    lax.fori_loop(0, 1, far_unit, 0)
                    far_table.wait()
                    rf0[...] = lax.fori_loop(0, sb // 4, far_tiles, jnp.zeros((8, N), F32))
                    mass_pair.wait_recv()
                    mass_diagonal = send(tmass.at[1], tmass.at[3], partner)
                if h == hops - 1:
                    t_pair.wait_recv()
                    t_diagonal = send(t_raw.at[1], t_raw.at[3], partner)
                    norm_t(1)
                    t_diagonal.wait_recv()
                    norm_t(3)
                    builds(0, first + places, (1, 3), False, True)
                if final:
                    builds(first, places, range(TARGETS), True, True)
        if final:
            compact(hops)
            norm_lines(2 * (nz - 1), 1)
            table_copy(hops).start()
            table_copy(hops).wait()
            last_build(0)
        for dz in (-h, h)[: 1 if final else 2]:
            post[dz].wait_recv()
    norm_lines(2 * nz - 1, 1)
    last_build(1)

    others = [(dz, bx) for dz in range(nz) for bx in range(2) if (dz, bx) != (0, 0)]
    others.sort(key=lambda o: -min(o[0], nz - o[0]))

    def exchange(src, dst, k, to_dev):
        return pltpu.make_async_remote_copy(
            src_ref=src, dst_ref=dst, send_sem=ex_snd.at[k], recv_sem=ex_rcv.at[k],
            device_id=to_dev, device_id_type=MESH)

    def group(j):
        return (lax.rem(nz - j, nz), j), (j + 1, j + 1)

    def spread(v, r):
        h, l = halves(v)
        return jnp.where(sub16 == r, h, jnp.where(sub16 == r + 8, l, 0.0)).astype(BF16)

    def product(lhs, tiles):
        o = nn(jnp.concatenate([v for v in lhs for _ in range(2)], axis=1), tiles)
        return o[:8] + o[8:]

    def rows_pass(rp, rpi, rf):
        def body(r0, _):
            j = hops - 1 - r0
            for dz, dist in group(j):
                for bx in range(2):
                    r = dz * 2 + bx
                    lhs = []
                    for t in range(TARGETS):
                        for u in range(CAP):
                            b, q = tabs_sm[dist, u, lane_of(r, t)], tabs_sm[dist, CAP + u, lane_of(r, t)]
                            lhs.append(spread(ts[t, pl.ds(jnp.maximum(q, 0), 1), :], b))
                    rp[r] = product(lhs, k_row[r])
            for dz, _ in group(j):
                send_rows(rp, rpi, dz)
            return 0

        lax.fori_loop(0, hops, body, 0)
        lhs = [spread(ts[0, pl.ds(tabf_sm[2 * CAP, f], 1), :], f) for f in range(sb)]
        rf[...] = product(lhs, kf_row[...])

    def cols_pass(so, ss, sf, far_copy):
        def body(j, accs):
            accs = list(accs)
            for dz, _ in group(j):
                for bx in range(2):
                    copy = from_line(so, ss, ag_snd, ag_rcv, dz, bx, True)
                    if bx == 0:
                        pl.when(dz > 0)(copy.wait_recv)
                    else:
                        copy.wait_recv()
            for dz, _ in group(j):
                for bx in range(2):
                    ssl[dz * 2 + bx] = ss[dz * 2 + bx]
            slots = [(t, u) for t in range(TARGETS) for u in range(CAP)]
            for dz, dist in group(j):
                for bx in range(2):
                    r = dz * 2 + bx
                    lhs = []
                    for k, (t, u) in enumerate(slots):
                        b = tabs_sm[dist, u, lane_of(r, t)]
                        lhs.append(spread(ssl[r, pl.ds(jnp.maximum(b, 0), 1), :], k))
                    o = product(lhs, k_col[r])
                    for k, (t, u) in enumerate(slots):
                        q = tabs_sm[dist, CAP + u, lane_of(r, t)]
                        accs[t] = accs[t] + jnp.where(sub32 == q, o[k : k + 1], 0.0)
            return tuple(accs)

        zero = jnp.zeros((tb_dev, N), F32)
        accs = list(lax.fori_loop(0, hops, body, (zero,) * TARGETS))
        far_copy.wait_recv()
        lhs = [spread(sf[f : f + 1, :], f) for f in range(sb)]
        o = product(lhs, kf_col[...])
        for f in range(sb):
            accs[0] = accs[0] + jnp.where(sub32 == tabf_sm[2 * CAP, f], o[f : f + 1], 0.0)
        return accs

    mass_core.wait_recv()
    mass_diagonal.wait_recv()
    for it, (rp, rpi, rf, rfi, so, ss, sf, co, ci, wo, wi) in enumerate((
        (rp0, rpi0, rf0, rfi0, so0, ss0, sf0, co0, ci0, wo0, wi0),
        (rp1, rpi1, rf1, rfi1, so1, ss1, sf1, co1, ci1, wo1, wi1),
    )):
        last = it == ITERS - 1
        far_rows = exchange(rf, rfi, 0, behind)
        far_scale = exchange(so, sf, 1, ahead)
        if it > 0:
            rows_pass(rp, rpi, rf)
        far_rows.start()
        total = rp[0]
        for o in others[::-1]:
            from_line(rp, rpi, rs_snd, rs_rcv, *o).wait_recv()
        far_rows.wait_recv()
        total = total + rfi[...]
        for o in others:
            total = total + rpi[rel(*o)]
        scale = smass[...] / (DUSTBIN + total)
        so[...] = scale
        ss[0] = scale
        if last:
            out[:sb] = scale
        for o in others:
            to_line(so, ss, ag_snd, ag_rcv, *o, True).start()
        far_scale.start()
        accs = cols_pass(so, ss, sf, far_scale)
        theirs = pl.ds(2, 2) if last else pl.ds(0, TARGETS)
        for t in range(2 if last else 0, TARGETS):
            co[t] = accs[t]
        cores = exchange(co.at[theirs], ci.at[theirs], 2 + 2 * it, partner)
        cores.start()
        for left, sem in ((rp, rs_snd), (ss, ag_snd)):
            pltpu.make_async_copy(left.at[pl.ds(1, nr - 1)], left.at[pl.ds(1, nr - 1)], sem.at[0]).wait()
        far_rows.wait_send()
        far_scale.wait_send()
        cores.wait_recv()
        sums = [accs[t] + ci[t ^ 2] for t in range(2 if last else TARGETS)]
        moving = pl.ds(1, 1) if last else pl.ds(0, TARGETS)
        for t in (1,) if last else range(TARGETS):
            wo[t] = sums[t]
        swap = exchange(wo.at[moving], wi.at[moving], 3 + 2 * it, pair)
        swap.start()
        swap.wait_recv()
        if last:
            out[sb:] = tmass[0] / (DUSTBIN + (sums[0] + wi[1]))
        else:
            for t in range(TARGETS):
                ts[t] = tmass[t] / (DUSTBIN + (sums[t] + wi[t ^ 1]))
        cores.wait_send()
        swap.wait_send()
    for copy in sent:
        copy.wait_send()
    assert count[0] == COPIES


def local(ng, nz, semb, temb, smass, tmass, cdev, cblk):
    sb, tb = semb.shape[0], temb.shape[0]
    nr = 2 * nz
    slots = TARGETS * CAP * 2 * N
    vm = pltpu.VMEM
    dma = pltpu.SemaphoreType.DMA
    tile = (N, N)
    blocks = vm((nr, sb, N), F32)
    source, targets = vm((sb, N), F32), vm((TARGETS, tb, N), F32)
    scratch = [
        vm((nr, sb) + tile, F32), vm((TARGETS, tb) + tile, F32), vm((sb,) + tile, F32),
        vm((nr * sb,) + tile, BF16), vm((nr * sb,) + tile, BF16),
        vm((TARGETS, tb) + tile, BF16), vm((TARGETS, tb) + tile, BF16),
        vm((sb,) + tile, BF16), vm((sb,) + tile, BF16),
        vm((nr, slots, N), BF16), vm((nr, slots, N), BF16),
        vm((sb * 2 * N, N), BF16), vm((sb * 2 * N, N), BF16),
        vm((8, N), I32), vm((nr, 8, N), I32), vm((8, N), I32), vm((nz // 2 + 1, 8, N), I32),
        pltpu.SMEM((nz // 2 + 1, 8, N), I32), pltpu.SMEM((8, N), I32),
    ]
    scratch += [blocks] * 7 + [source] * 8 + [targets] * 9
    scratch += [vm(a.shape, a.dtype) for a in (smass, cdev, cblk)] + [targets]
    scratch += [dma((COPIES,))] * 2 + [dma((1,)), dma((nr,)), dma((1,)), dma((nr,))] + [dma((6,))] * 2 + [dma((8,))]
    any_, vmem = pl.BlockSpec(memory_space=pl.ANY), pl.BlockSpec(memory_space=pltpu.VMEM)
    both = pl.pallas_call(
        functools.partial(kernel, ng, nz, sb, tb),
        out_shape=jax.ShapeDtypeStruct((sb + tb, N), F32),
        in_specs=[any_] * 6,
        out_specs=vmem,
        scratch_shapes=scratch,
        compiler_params=pltpu.CompilerParams(
            collective_id=0, has_side_effects=True, vmem_limit_bytes=VMEM_BYTES),
        name="sinkhorn",
    )(semb, temb, smass, tmass, cdev, cblk)

    def split(both_ref, src_ref, tgt_ref):
        src_ref[...] = both_ref[:sb]
        tgt_ref[...] = both_ref[sb:]

    return pl.pallas_call(
        split,
        out_shape=(jax.ShapeDtypeStruct(smass.shape, F32), jax.ShapeDtypeStruct(tmass.shape, F32)),
        in_specs=[vmem],
        out_specs=(vmem, vmem),
        name="split",
    )(both)


def solution(mesh):
    placed = (
        P(("group", "dev"), None, None),
        P(("group", "dev"), None, None),
        P(("group", "dev"), None),
        P(("group", "dev"), None),
        P(("group", "dev"), None),
        P(("group", "dev"), None),
    )
    ng, nz = mesh.shape["group"], mesh.shape["dev"] // (2 * NX)
    return jax.shard_map(
        functools.partial(local, ng, nz),
        mesh=mesh,
        in_specs=placed,
        out_specs=(P(("group", "dev"), None), P(("group", "dev"), None)),
        check_vma=False,
    )
```

time: 113 us -> 110 us (0.973)
  Pallas kernels: 113 us -> 109 us
    pallas_call x1, Pallas kernels: 111 us -> 108 us  [local(): pl.pallas_call(functools.partial(kernel, ng, nz, sb, tb), out_shape=jax.S...]
where the time goes in v6:
time: 110 us
  Pallas kernels  109 us (99%)
    pallas_call x1, Pallas kernels, local(): pl.pallas_call(functools.partial(kernel, ng, nz, sb, tb), out_shape=jax.S...  108 us

profile of v6, /device:TPU:1, one launch (start us, length us, event | category | flops | bytes accessed | tf_op | source)
XLA Modules:
  0.0 110.0 jit_solution(6856044205701569485)
XLA Ops:
  0.6 108.1 %sinkhorn.1.both_ref = f32[40,128]{1,0:T(8,128)} custom-call(f32[8,128,128]{2,1,0:T(8,128)} %refs_0_.1, f32[32,128,128]{2,1,0:T(8,128)} %refs_1_.1, f32[8,128]{1,0:T(8,128)} %refs_2_.1, f32[32,128]{1,0:T(8,128)} %refs_3_.1, s32[8,7]{1,0:T(8,128)} %refs_4_.1, s32[8,8]{1,0:T(8,128)} %refs_5_.1), custom_call_target="tpu_custom_call" | custom-call | tf_op jit(solution)/shard_map/sinkhorn/pallas_call | solution.py:494
  108.7 1.3 %split.1 = (f32[8,128]{1,0:T(8,128)}, f32[32,128]{1,0:T(8,128)}) custom-call(f32[40,128]{1,0:T(8,128)} %sinkhorn.1.both_ref), custom_call_target="tpu_custom_call" | custom-call | tf_op jit(solution)/shard_map/split/pallas_call | solution.py:509

commit v7 on v6

--- a/solution.py
+++ b/solution.py
@@ -283,10 +283,15 @@
         for p in range(3):
             for k, (dz, got, onward) in enumerate(((-h, z_plus, up), (h, z_minus, down))):
                 got[h, p].wait_recv()
+                if h + 2 == hops and p == 2:
+                    continue
                 if h + 1 < hops:
                     got[h + 1, p] = send(piece(dz, p), piece(-h - 1 if k == 0 else h + 1, p), onward)
                 elif h + 1 == hops:
                     got[hops, p] = send(piece(dz, p, k * quarter, quarter), piece(hops, p, k * quarter, quarter), onward)
+            if h + 1 == hops and p == 0:
+                z_plus[h, 2] = send(piece(1 - h, 2), piece(-h, 2), up)
+                z_minus[h, 2] = send(piece(h - 1, 2), piece(h, 2), down)
             if p == 0:
                 for dz in (-h, h)[: 1 if final else 2]:
                     post[dz] = send(s_raw.at[rel(dz, 0), hi], s_raw.at[rel(dz, 1), hi], mate)
@@ -324,13 +329,13 @@
                     norm_t(3)
                     builds(0, first + places, (1, 3), False, True)
                 if final:
+                    compact(hops)
                     builds(first, places, range(TARGETS), True, True)
-        if final:
-            compact(hops)
-            norm_lines(2 * (nz - 1), 1)
-            table_copy(hops).start()
-            table_copy(hops).wait()
-            last_build(0)
+                    table_copy(hops).start()
+            if final and p == 1:
+                table_copy(hops).wait()
+                norm_lines(2 * (nz - 1), 1)
+                last_build(0)
         for dz in (-h, h)[: 1 if final else 2]:
             post[dz].wait_recv()
     norm_lines(2 * nz - 1, 1)

time: 110 us -> 110 us (level)
  no operation moved by 1% of the time
where the time goes in v7:
time: 110 us
  Pallas kernels  109 us (99%)
    pallas_call x1, Pallas kernels, local(): pl.pallas_call(functools.partial(kernel, ng, nz, sb, tb), out_shape=jax.S...  108 us

profile of v7, /device:TPU:1, one launch (start us, length us, event | category | flops | bytes accessed | tf_op | source)
XLA Modules:
  0.0 110.1 jit_solution(11585141100220107190)
XLA Ops:
  0.6 108.1 %sinkhorn.1.both_ref = f32[40,128]{1,0:T(8,128)} custom-call(f32[8,128,128]{2,1,0:T(8,128)} %refs_0_.1, f32[32,128,128]{2,1,0:T(8,128)} %refs_1_.1, f32[8,128]{1,0:T(8,128)} %refs_2_.1, f32[32,128]{1,0:T(8,128)} %refs_3_.1, s32[8,7]{1,0:T(8,128)} %refs_4_.1, s32[8,8]{1,0:T(8,128)} %refs_5_.1), custom_call_target="tpu_custom_call" | custom-call | tf_op jit(solution)/shard_map/sinkhorn/pallas_call | solution.py:499
  108.7 1.3 %split.1 = (f32[8,128]{1,0:T(8,128)}, f32[32,128]{1,0:T(8,128)}) custom-call(f32[40,128]{1,0:T(8,128)} %sinkhorn.1.both_ref), custom_call_target="tpu_custom_call" | custom-call | tf_op jit(solution)/shard_map/split/pallas_call | solution.py:514

commit v8 on v6

--- a/solution.py
+++ b/solution.py
@@ -272,67 +272,90 @@
             acc = acc + jnp.where(sub8 == f, sums, 0.0)
         return acc
 
-    for h in range(1, hops + 1):
-        final = h == hops
+    def take_tables(h):
         w_plus[h].wait_recv()
-        if not final:
+        if h < hops:
             w_plus[h + 1] = send(two(-h), two(-h - 1), up)
             w_minus[h].wait_recv()
             if h + 1 < hops:
                 w_minus[h + 1] = send(two(h), two(h + 1), down)
-        for p in range(3):
-            for k, (dz, got, onward) in enumerate(((-h, z_plus, up), (h, z_minus, down))):
-                got[h, p].wait_recv()
-                if h + 1 < hops:
-                    got[h + 1, p] = send(piece(dz, p), piece(-h - 1 if k == 0 else h + 1, p), onward)
-                elif h + 1 == hops:
-                    got[hops, p] = send(piece(dz, p, k * quarter, quarter), piece(hops, p, k * quarter, quarter), onward)
-            if p == 0:
-                for dz in (-h, h)[: 1 if final else 2]:
-                    post[dz] = send(s_raw.at[rel(dz, 0), hi], s_raw.at[rel(dz, 1), hi], mate)
-            if p == (0 if final else 1):
-                dist = h - 1
-                first, places = (0, 1) if dist == 0 else (2 * dist - 1, 2)
-                compact(dist)
-                norm_lines(2 * first, places)
-                table_copy(dist).start()
-                norm_lines(2 * first + places, places)
-                table_copy(dist).wait()
-                if not final:
-                    builds(first, places, (0, 2), True, False)
-                if h == 2:
-                    w_far.wait_recv()
-                    far_table = pltpu.make_async_copy(tabf, tabf_sm, loc.at[3])
-                    far_table.start()
-                    f_far.wait_recv()
-
-                    def far_unit(i, _):
-                        for w in range(sb):
-                            f_hi[w], f_lo[w] = unit(f_raw[w], True)
-                        return 0
-
-                    lax.fori_loop(0, 1, far_unit, 0)
-                    far_table.wait()
-                    rf0[...] = lax.fori_loop(0, sb // 4, far_tiles, jnp.zeros((8, N), F32))
-                    mass_pair.wait_recv()
-                    mass_diagonal = send(tmass.at[1], tmass.at[3], partner)
-                if h == hops - 1:
-                    t_pair.wait_recv()
-                    t_diagonal = send(t_raw.at[1], t_raw.at[3], partner)
-                    norm_t(1)
-                    t_diagonal.wait_recv()
-                    norm_t(3)
-                    builds(0, first + places, (1, 3), False, True)
-                if final:
-                    builds(first, places, range(TARGETS), True, True)
-        if final:
-            compact(hops)
-            norm_lines(2 * (nz - 1), 1)
-            table_copy(hops).start()
-            table_copy(hops).wait()
-            last_build(0)
-        for dz in (-h, h)[: 1 if final else 2]:
+
+    def take(h, p):
+        for k, (dz, got, onward) in enumerate(((-h, z_plus, up), (h, z_minus, down))):
+            got[h, p].wait_recv()
+            if h + 2 == hops and p == 2:
+                continue
+            if h + 1 < hops:
+                got[h + 1, p] = send(piece(dz, p), piece(-h - 1 if k == 0 else h + 1, p), onward)
+            elif h + 1 == hops:
+                got[hops, p] = send(piece(dz, p, k * quarter, quarter), piece(hops, p, k * quarter, quarter), onward)
+        if h + 1 == hops and p == 0:
+            z_plus[h, 2] = send(piece(1 - h, 2), piece(-h, 2), up)
+            z_minus[h, 2] = send(piece(h - 1, 2), piece(h, 2), down)
+        if p == 0:
+            for dz in (-h, h)[: 1 if h == hops else 2]:
+                post[dz] = send(s_raw.at[rel(dz, 0), hi], s_raw.at[rel(dz, 1), hi], mate)
+
+    def take_post(h):
+        for dz in (-h, h)[: 1 if h == hops else 2]:
             post[dz].wait_recv()
+
+    def lines_of(dist):
+        return (0, 1) if dist == 0 else (2 * dist - 1, 2)
+
+    def bring(dist):
+        first, places = lines_of(dist)
+        compact(dist)
+        norm_lines(2 * first, places)
+        table_copy(dist).start()
+        norm_lines(2 * first + places, places)
+        table_copy(dist).wait()
+
+    for h in range(1, hops):
+        take_tables(h)
+        take(h, 0)
+        take(h, 1)
+        bring(h - 1)
+        builds(*lines_of(h - 1), (0, 2), True, False)
+        if h == 2:
+            w_far.wait_recv()
+            far_table = pltpu.make_async_copy(tabf, tabf_sm, loc.at[3])
+            far_table.start()
+            f_far.wait_recv()
+
+            def far_unit(i, _):
+                for w in range(sb):
+                    f_hi[w], f_lo[w] = unit(f_raw[w], True)
+                return 0
+
+            lax.fori_loop(0, 1, far_unit, 0)
+            far_table.wait()
+            rf0[...] = lax.fori_loop(0, sb // 4, far_tiles, jnp.zeros((8, N), F32))
+            mass_pair.wait_recv()
+            mass_diagonal = send(tmass.at[1], tmass.at[3], partner)
+        if h < hops - 1:
+            take(h, 2)
+            take_post(h)
+    t_pair.wait_recv()
+    t_diagonal = send(t_raw.at[1], t_raw.at[3], partner)
+    norm_t(1)
+    take_tables(hops)
+    take(hops, 0)
+    t_diagonal.wait_recv()
+    norm_t(3)
+    builds(0, 2 * hops - 3, (1, 3), False, True)
+    take(hops - 1, 2)
+    take_post(hops - 1)
+    bring(hops - 1)
+    compact(hops)
+    builds(*lines_of(hops - 1), range(TARGETS), True, True)
+    table_copy(hops).start()
+    take(hops, 1)
+    table_copy(hops).wait()
+    norm_lines(2 * (nz - 1), 1)
+    last_build(0)
+    take(hops, 2)
+    take_post(hops)
     norm_lines(2 * nz - 1, 1)
     last_build(1)
 

time: 110 us -> 110 us (level)
  no operation moved by 1% of the time
where the time goes in v8:
time: 110 us
  Pallas kernels  109 us (99%)
    pallas_call x1, Pallas kernels, local(): pl.pallas_call(functools.partial(kernel, ng, nz, sb, tb), out_shape=jax.S...  108 us

profile of v8, /device:TPU:1, one launch (start us, length us, event | category | flops | bytes accessed | tf_op | source)
XLA Modules:
  0.0 109.8 jit_solution(7124294464336235998)
XLA Ops:
  0.6 107.8 %sinkhorn.1.both_ref = f32[40,128]{1,0:T(8,128)} custom-call(f32[8,128,128]{2,1,0:T(8,128)} %refs_0_.1, f32[32,128,128]{2,1,0:T(8,128)} %refs_1_.1, f32[8,128]{1,0:T(8,128)} %refs_2_.1, f32[32,128]{1,0:T(8,128)} %refs_3_.1, s32[8,7]{1,0:T(8,128)} %refs_4_.1, s32[8,8]{1,0:T(8,128)} %refs_5_.1), custom_call_target="tpu_custom_call" | custom-call | tf_op jit(solution)/shard_map/sinkhorn/pallas_call | solution.py:517
  108.5 1.3 %split.1 = (f32[8,128]{1,0:T(8,128)}, f32[32,128]{1,0:T(8,128)}) custom-call(f32[40,128]{1,0:T(8,128)} %sinkhorn.1.both_ref), custom_call_target="tpu_custom_call" | custom-call | tf_op jit(solution)/shard_map/split/pallas_call | solution.py:532

commit v9 on v8

--- a/solution.py
+++ b/solution.py
@@ -64,16 +64,21 @@
     ahead, behind = (lax.rem(g + 1, ng), d), (lax.rem(g + ng - 1, ng), d)
 
     count = [0]
-    sent = []
+
+    def kind(src):
+        if src.dtype == I32:
+            return 2
+        if len(src.shape) == 2:
+            return 3
+        return 1 if src.shape[0] == tb_dev else 0
 
     def send(src, dst, to_dev):
         k = count[0]
         count[0] += 1
         copy = pltpu.make_async_remote_copy(
-            src_ref=src, dst_ref=dst, send_sem=snd.at[k], recv_sem=rcv.at[k],
+            src_ref=src, dst_ref=dst, send_sem=snd.at[kind(src)], recv_sem=rcv.at[k],
             device_id=to_dev, device_id_type=MESH)
         copy.start()
-        sent.append(copy)
         return copy
 
     barrier = pltpu.get_barrier_semaphore()
@@ -426,13 +431,13 @@
             return tuple(accs)
 
         zero = jnp.zeros((tb_dev, N), F32)
-        accs = list(lax.fori_loop(0, hops, body, (zero,) * TARGETS))
+        first = zero
         far_copy.wait_recv()
         lhs = [spread(sf[f : f + 1, :], f) for f in range(sb)]
         o = product(lhs, kf_col[...])
         for f in range(sb):
-            accs[0] = accs[0] + jnp.where(sub32 == tabf_sm[2 * CAP, f], o[f : f + 1], 0.0)
-        return accs
+            first = first + jnp.where(sub32 == tabf_sm[2 * CAP, f], o[f : f + 1], 0.0)
+        return list(lax.fori_loop(0, hops, body, (first,) + (zero,) * (TARGETS - 1)))
 
     mass_core.wait_recv()
     mass_diagonal.wait_recv()
@@ -486,8 +491,9 @@
                 ts[t] = tmass[t] / (DUSTBIN + (sums[t] + wi[t ^ 1]))
         cores.wait_send()
         swap.wait_send()
-    for copy in sent:
-        copy.wait_send()
+    others_part = pl.ds(1, TARGETS - 1)
+    for k, left in enumerate((s_raw, t_raw.at[others_part], tabs, tmass.at[others_part])):
+        pltpu.make_async_copy(left, left, snd.at[k]).wait()
     assert count[0] == COPIES
 
 
@@ -512,7 +518,7 @@
     ]
     scratch += [blocks] * 7 + [source] * 8 + [targets] * 9
     scratch += [vm(a.shape, a.dtype) for a in (smass, cdev, cblk)] + [targets]
-    scratch += [dma((COPIES,))] * 2 + [dma((1,)), dma((nr,)), dma((1,)), dma((nr,))] + [dma((6,))] * 2 + [dma((8,))]
+    scratch += [dma((4,)), dma((COPIES,)), dma((1,)), dma((nr,)), dma((1,)), dma((nr,))] + [dma((6,))] * 2 + [dma((8,))]
     any_, vmem = pl.BlockSpec(memory_space=pl.ANY), pl.BlockSpec(memory_space=pltpu.VMEM)
     both = pl.pallas_call(
         functools.partial(kernel, ng, nz, sb, tb),

time: 110 us -> 109 us (level)
  no operation moved by 1% of the time
where the time goes in v9:
time: 109 us
  Pallas kernels  108 us (99%)
    pallas_call x1, Pallas kernels, local(): pl.pallas_call(functools.partial(kernel, ng, nz, sb, tb), out_shape=jax.S...  107 us

profile of v9, /device:TPU:1, one launch (start us, length us, event | category | flops | bytes accessed | tf_op | source)
XLA Modules:
  0.0 109.1 jit_solution(14086320551406586437)
XLA Ops:
  0.6 107.1 %sinkhorn.1.both_ref = f32[40,128]{1,0:T(8,128)} custom-call(f32[8,128,128]{2,1,0:T(8,128)} %refs_0_.1, f32[32,128,128]{2,1,0:T(8,128)} %refs_1_.1, f32[8,128]{1,0:T(8,128)} %refs_2_.1, f32[32,128]{1,0:T(8,128)} %refs_3_.1, s32[8,7]{1,0:T(8,128)} %refs_4_.1, s32[8,8]{1,0:T(8,128)} %refs_5_.1), custom_call_target="tpu_custom_call" | custom-call | tf_op jit(solution)/shard_map/sinkhorn/pallas_call | solution.py:523
  107.8 1.3 %split.1 = (f32[8,128]{1,0:T(8,128)}, f32[32,128]{1,0:T(8,128)}) custom-call(f32[40,128]{1,0:T(8,128)} %sinkhorn.1.both_ref), custom_call_target="tpu_custom_call" | custom-call | tf_op jit(solution)/shard_map/split/pallas_call | solution.py:538

commit v10 on v9

--- a/solution.py
+++ b/solution.py
@@ -185,7 +185,6 @@
     t_core.wait_recv()
     norm_t(2)
     own_s.wait()
-    post[0].wait_recv()
 
     sub8 = lax.broadcasted_iota(I32, (8, N), 0)
     sub16 = lax.broadcasted_iota(I32, (16, N), 0)
@@ -317,9 +316,11 @@
         table_copy(dist).wait()
 
     for h in range(1, hops):
+        take(h, 0)
         take_tables(h)
-        take(h, 0)
         take(h, 1)
+        if h == 1:
+            post[0].wait_recv()
         bring(h - 1)
         builds(*lines_of(h - 1), (0, 2), True, False)
         if h == 2:
@@ -344,8 +345,8 @@
     t_pair.wait_recv()
     t_diagonal = send(t_raw.at[1], t_raw.at[3], partner)
     norm_t(1)
+    take(hops, 0)
     take_tables(hops)
-    take(hops, 0)
     t_diagonal.wait_recv()
     norm_t(3)
     builds(0, 2 * hops - 3, (1, 3), False, True)

time: 109 us -> 109 us (level)
  no operation moved by 1% of the time
where the time goes in v10:
time: 109 us
  Pallas kernels  109 us (100%)
    pallas_call x1, Pallas kernels, local(): pl.pallas_call(functools.partial(kernel, ng, nz, sb, tb), out_shape=jax.S...  107 us

profile of v10, /device:TPU:1, one launch (start us, length us, event | category | flops | bytes accessed | tf_op | source)
XLA Modules:
  0.0 109.2 jit_solution(7603820816548361717)
XLA Ops:
  0.6 107.2 %sinkhorn.1.both_ref = f32[40,128]{1,0:T(8,128)} custom-call(f32[8,128,128]{2,1,0:T(8,128)} %refs_0_.1, f32[32,128,128]{2,1,0:T(8,128)} %refs_1_.1, f32[8,128]{1,0:T(8,128)} %refs_2_.1, f32[32,128]{1,0:T(8,128)} %refs_3_.1, s32[8,7]{1,0:T(8,128)} %refs_4_.1, s32[8,8]{1,0:T(8,128)} %refs_5_.1), custom_call_target="tpu_custom_call" | custom-call | tf_op jit(solution)/shard_map/sinkhorn/pallas_call | solution.py:524
  107.9 1.3 %split.1 = (f32[8,128]{1,0:T(8,128)}, f32[32,128]{1,0:T(8,128)}) custom-call(f32[40,128]{1,0:T(8,128)} %sinkhorn.1.both_ref), custom_call_target="tpu_custom_call" | custom-call | tf_op jit(solution)/shard_map/split/pallas_call | solution.py:539

commit v11 on v9

--- a/solution.py
+++ b/solution.py
@@ -406,18 +406,16 @@
     def cols_pass(so, ss, sf, far_copy):
         def body(j, accs):
             accs = list(accs)
-            for dz, _ in group(j):
+            slots = [(t, u) for t in range(TARGETS) for u in range(CAP)]
+            for dz, dist in group(j):
                 for bx in range(2):
                     copy = from_line(so, ss, ag_snd, ag_rcv, dz, bx, True)
                     if bx == 0:
                         pl.when(dz > 0)(copy.wait_recv)
                     else:
                         copy.wait_recv()
-            for dz, _ in group(j):
                 for bx in range(2):
                     ssl[dz * 2 + bx] = ss[dz * 2 + bx]
-            slots = [(t, u) for t in range(TARGETS) for u in range(CAP)]
-            for dz, dist in group(j):
                 for bx in range(2):
                     r = dz * 2 + bx
                     lhs = []

time: 109 us -> 109 us (level)
  no operation moved by 1% of the time
where the time goes in v11:
time: 109 us
  Pallas kernels  109 us (100%)
    pallas_call x1, Pallas kernels, local(): pl.pallas_call(functools.partial(kernel, ng, nz, sb, tb), out_shape=jax.S...  107 us

profile of v11, /device:TPU:1, one launch (start us, length us, event | category | flops | bytes accessed | tf_op | source)
XLA Modules:
  0.0 109.3 jit_solution(341123303027162203)
XLA Ops:
  0.6 107.3 %sinkhorn.1.both_ref = f32[40,128]{1,0:T(8,128)} custom-call(f32[8,128,128]{2,1,0:T(8,128)} %refs_0_.1, f32[32,128,128]{2,1,0:T(8,128)} %refs_1_.1, f32[8,128]{1,0:T(8,128)} %refs_2_.1, f32[32,128]{1,0:T(8,128)} %refs_3_.1, s32[8,7]{1,0:T(8,128)} %refs_4_.1, s32[8,8]{1,0:T(8,128)} %refs_5_.1), custom_call_target="tpu_custom_call" | custom-call | tf_op jit(solution)/shard_map/sinkhorn/pallas_call | solution.py:521
  108.0 1.3 %split.1 = (f32[8,128]{1,0:T(8,128)}, f32[32,128]{1,0:T(8,128)}) custom-call(f32[40,128]{1,0:T(8,128)} %sinkhorn.1.both_ref), custom_call_target="tpu_custom_call" | custom-call | tf_op jit(solution)/shard_map/split/pallas_call | solution.py:536
